TPU v7x, 32 devices: a whole 2x2x4 slice. The times are simulated.
32 devices in a mesh: dp: 8 (over z, x), tensor: 4 (over y, core).
Axes of the slice: x: 2, y: 2, z: 4, core: 2. Of those that a mesh axis runs over, the one named last changes fastest.
Arguments:
- inputs: bfloat16 [16, 1024, 1024], P('dp'), may hold values from -6 to 6
- segment_ids: int32 [16, 1024], P('dp'), may hold values from 0 to 7, never falling along the last dimension, each value on 1 to 512 neighbouring positions
- doc_offsets: int32 [16, 8], P('dp'), may hold values from 0 to 3071
- time_index: int32 [16], P('dp'), may hold values from 0 to 999
- w_qkv: bfloat16 [3, 1024, 1024], P(None, 'dp', 'tensor'), may hold values from -0.1875 to 0.1875
- w_out: bfloat16 [1024, 1024], P('tensor', 'dp'), may hold values from -0.75 to 0.75
- w_up: bfloat16 [1024, 4096], P('dp', 'tensor'), may hold values from -0.1875 to 0.1875
- w_down: bfloat16 [4096, 1024], P('tensor', 'dp'), may hold values from -0.09375 to 0.09375
- w_time: bfloat16 [256, 1024], P(None, 'dp'), may hold values from -0.375 to 0.375
- gain_attn: bfloat16 [1024], P('dp'), may hold values from 0.5 to 1.5
- gain_mlp: bfloat16 [1024], P('dp'), may hold values from 0.5 to 1.5
- cotangent: bfloat16 [16, 1024, 1024], P('dp'), may hold values from -6 to 6
Outputs:
- block_out: bfloat16 [16, 1024, 1024], P('dp', None, 'tensor')
- input_grad: float32 [16, 1024, 1024], P('dp', None, 'tensor')
- grad_qkv: float32 [3, 1024, 1024], P(None, 'dp', 'tensor')
- grad_out: float32 [1024, 1024], P('tensor', 'dp')
- grad_up: float32 [1024, 4096], P('dp', 'tensor')
- grad_down: float32 [4096, 1024], P('tensor', 'dp')
- grad_time: float32 [256, 1024], P(None, 'dp')
- grad_gain_attn: float32 [1024], P('dp')
- grad_gain_mlp: float32 [1024], P('dp')
Inputs may be any that keep to these rules, and one draw needn't show every extreme that they name: `segment_ids`: in each sequence the ids never fall, every id of 0 to 7 occurs, each document has 1 to 512 tokens and one has exactly 512.
All inputs are finite; a program needn't handle non-finite values.
Results may differ from a plain program's by a relative error of at most 0.022.
Values may be sent and summed in bfloat16 or wider, within the bound.
No kernel may reach another device: no remote copies, remote signals or barrier semaphores. Data moves between devices by JAX's collectives and lax.ppermute only.
A program may use at most 192 MiB of HBM per device.

v0:
```python
import math
import jax
import jax.numpy as jnp
from jax import lax
from jax.sharding import PartitionSpec as P

HEADS = 16
TEMB = 256
eps = 1e-05
masked = -1000000000.0
f32 = jnp.float32
bf16 = jnp.bfloat16


def sinusoid(values, width):
    half = width // 2
    freqs = jnp.exp(-math.log(10000.0) * jnp.arange(half, dtype=f32) / half)
    angles = values[..., None] * freqs
    return jnp.concatenate([jnp.sin(angles), jnp.cos(angles)], axis=-1)


def norm_parts(hidden):
    centre = jnp.mean(hidden, axis=-1, keepdims=True)
    centred = hidden - centre
    spread = jnp.mean(centred * centred, axis=-1, keepdims=True)
    inv = lax.rsqrt(spread + eps)
    return (centred * inv, inv)


def norm_back(unit, inv, gain, grad):
    scaled = grad * gain
    first = jnp.mean(scaled, axis=-1, keepdims=True)
    second = jnp.mean(scaled * unit, axis=-1, keepdims=True)
    return inv * (scaled - first - unit * second)


def positions(segs, offsets):
    seq_len = segs.shape[0]
    index = jnp.arange(seq_len, dtype=jnp.int32)
    member = segs[:, None] == jnp.arange(offsets.shape[0], dtype=jnp.int32)[None, :]
    starts = jnp.min(jnp.where(member, index[:, None], seq_len), axis=0)
    start_tok = jnp.sum(jnp.where(member, starts[None, :], 0), axis=1)
    offset_tok = jnp.sum(jnp.where(member, offsets[None, :], 0), axis=1)
    return offset_tok + index - start_tok


def attend(query, key, value, same, scale):
    scores = jnp.einsum("qhe,khe->hqk", query, key, preferred_element_type=f32) * scale
    scores = jnp.where(same[None], scores, masked)
    top = jnp.max(scores, axis=-1, keepdims=True)
    expo = jnp.exp(scores - top)
    denom = jnp.sum(expo, axis=-1, keepdims=True)
    probs = (expo / denom).astype(bf16)
    out = jnp.einsum("hqk,khe->qhe", probs, value, preferred_element_type=f32)
    return (out, top + jnp.log(denom))


def attend_back(query, key, value, same, scale, lse, d_mixed):
    scores = jnp.einsum("qhe,khe->hqk", query, key, preferred_element_type=f32) * scale
    scores = jnp.where(same[None], scores, masked)
    probs = jnp.exp(scores - lse)
    d_probs = jnp.einsum("qhe,khe->hqk", d_mixed, value, preferred_element_type=f32)
    d_value = jnp.einsum("hqk,qhe->khe", probs.astype(bf16), d_mixed, preferred_element_type=f32)
    delta = jnp.sum(probs * d_probs, axis=-1, keepdims=True)
    d_scores = (probs * (d_probs - delta)).astype(bf16)
    d_query = jnp.einsum("hqk,khe->qhe", d_scores, key, preferred_element_type=f32) * scale
    d_key = jnp.einsum("hqk,qhe->khe", d_scores, query, preferred_element_type=f32) * scale
    return (d_query, d_key, d_value)


def mm(left, right):
    return jnp.dot(left, right, preferred_element_type=f32)


def mm_rt(left, right):
    return jnp.einsum("ik,jk->ij", left, right, preferred_element_type=f32)


def mm_lt(left, right):
    return jnp.einsum("ki,kj->ij", left, right, preferred_element_type=f32)


class Ring:

    def __init__(self, n):
        self.n = n
        self.order = list(range(0, n, 2)) + list(range(n - 1, 0, -2))
        inverse = [self.order.index(i) for i in range(n)]
        self.me = lax.axis_index("dp")
        self.spot = jnp.array(inverse, jnp.int32)[self.me]
        self.table = jnp.array(self.order, jnp.int32)
        self.right = [(self.order[p], self.order[(p + 1) % n]) for p in range(n)]
        self.left = [(b, a) for a, b in self.right]

    def at(self, offset):
        return self.table[(self.spot + offset) % self.n]

    def gather(self, block):
        rows = block.shape[0]
        full = jnp.zeros((self.n * rows,) + block.shape[1:], block.dtype)
        full = lax.dynamic_update_slice_in_dim(full, block, self.me * rows, 0)
        from_left = from_right = block
        for hop in range(1, self.n // 2 + 1):
            from_left = lax.ppermute(from_left, "dp", self.right)
            if hop <= self.n - 1 - self.n // 2:
                from_right = lax.ppermute(from_right, "dp", self.left)
                full = lax.dynamic_update_slice_in_dim(full, from_right, self.at(hop) * rows, 0)
            full = lax.dynamic_update_slice_in_dim(full, from_left, self.at(-hop) * rows, 0)
        return full

    def scatter(self, full):
        rows = full.shape[0] // self.n

        def part(offset):
            return lax.dynamic_slice_in_dim(full, self.at(offset) * rows, rows, 0).astype(f32)

        total = part(0)
        for hops, way, sign in (
            (self.n // 2, self.right, 1),
            (self.n - 1 - self.n // 2, self.left, -1),
        ):
            run = part(sign * hops)
            for hop in range(1, hops + 1):
                run = lax.ppermute(run.astype(bf16), "dp", way).astype(f32)
                if hop < hops:
                    run = run + part(sign * (hops - hop))
            if hops:
                total = total + run
        return total


def swap(value, bit, n):
    return lax.ppermute(value, "tensor", [(i, i ^ bit) for i in range(n)])


def to_features(value, n):
    me = lax.axis_index("tensor")
    tokens, width = value.shape
    value = value.reshape(tokens, n, width // n)
    bit = 1
    while bit < n:
        value = value.reshape(tokens, -1, 2, width // n)
        mine = me // bit % 2
        keep = lax.dynamic_index_in_dim(value, mine, 2, keepdims=False)
        send = lax.dynamic_index_in_dim(value, 1 - mine, 2, keepdims=False)
        got = swap(send.astype(bf16), bit, n).astype(f32)
        if bit == 1:
            got = jnp.concatenate([got[tokens // 2 :], got[: tokens // 2]], axis=0)
        value = keep.astype(f32) + got
        bit *= 2
    return value.reshape(tokens, width // n)


def shards(
    inputs,
    segment_ids,
    doc_offsets,
    time_index,
    w_qkv,
    w_out,
    w_up,
    w_down,
    w_time,
    gain_attn,
    gain_mlp,
    cotangent,
):
    n_dp = lax.axis_size("dp")
    n_tensor = lax.axis_size("tensor")
    me_dp = lax.axis_index("dp")
    core = lax.axis_index("tensor") % 2
    chips = n_tensor // 2
    seqs_dev, seq_len, width = inputs.shape
    half = seq_len // 2
    shard = width // n_tensor
    head_size = width // HEADS
    heads_dev = shard // head_size
    scale = head_size ** (-0.5)
    hidden_dev = w_up.shape[1]
    ring = Ring(n_dp)
    w1_part = jnp.concatenate([w_qkv[0], w_qkv[1], w_qkv[2], w_out.T], axis=1)
    w1 = ring.gather(w1_part)
    w2_part = jnp.concatenate([w_up, w_down.T], axis=1)
    w2 = lax.all_gather(w2_part, "dp", axis=0, tiled=True)
    times = lax.all_gather(time_index, "dp", axis=0, tiled=True)
    temb = sinusoid(times.astype(f32), TEMB)
    cond_part = jnp.dot(temb, w_time.astype(f32), precision=lax.Precision.HIGHEST)
    small = jnp.concatenate(
        [cond_part, gain_attn.astype(f32)[None], gain_mlp.astype(f32)[None]], axis=0
    )
    small = lax.all_gather(small, "dp", axis=1, tiled=True)
    n_seqs = n_dp * seqs_dev
    cond = lax.dynamic_slice_in_dim(small, me_dp * seqs_dev, seqs_dev, 0)
    attn_g, mlp_g = (small[n_seqs], small[n_seqs + 1])

    def own_first(value):
        return jnp.roll(value, -core * half, axis=0)

    def exchange_core(value):
        return swap(value, 1, n_tensor)

    def sum_chips(value):
        bit = 2
        value = value.astype(f32)
        while bit < n_tensor:
            low = value.astype(bf16)
            value = low.astype(f32) + swap(low, bit, n_tensor).astype(f32)
            bit *= 2
        return value

    seqs = range(seqs_dev)
    cot = [own_first(cotangent[i]) for i in seqs]
    segs = [own_first(segment_ids[i]) for i in seqs]
    same = [s[:, None] == s[None, :] for s in segs]
    h0, unit0, inv0, n1 = ([], [], [], [])
    for i in seqs:
        place = own_first(positions(segment_ids[i], doc_offsets[i]))
        h = own_first(inputs[i]).astype(f32) + sinusoid(place.astype(f32), width) + cond[i][None]
        unit, inv = norm_parts(h)
        h0.append(h)
        unit0.append(unit)
        inv0.append(inv)
        n1.append((unit * attn_g).astype(bf16))
    query, key, value, mixed, lse = ([], [], [], [], [])
    h1, unit1, inv1, n2 = ([], [], [], [])
    for i in seqs:
        qkv = mm(n1[i], w1[:, : 3 * shard]).astype(bf16)
        heads = [
            qkv[:, c * shard : (c + 1) * shard].reshape(seq_len, heads_dev, head_size)
            for c in range(3)
        ]
        out, total = attend(*heads, same[i], scale)
        out = out.reshape(seq_len, shard).astype(bf16)
        send = mm_rt(out[half:], w1[:, 3 * shard :]).astype(bf16)
        keep = mm_rt(out[:half], w1[:, 3 * shard :]).astype(bf16)
        attn = sum_chips(keep.astype(f32) + exchange_core(send).astype(f32))
        h = h0[i][:half] + attn
        unit, inv = norm_parts(h)
        own = (unit * mlp_g).astype(bf16)
        query.append(heads[0])
        key.append(heads[1])
        value.append(heads[2])
        mixed.append(out)
        lse.append(total)
        h1.append(h)
        unit1.append(unit)
        inv1.append(inv)
        n2.append(jnp.concatenate([own, exchange_core(own)], axis=0))
    w_up_full, w_down_t = (w2[:, :hidden_dev], w2[:, hidden_dev:])
    active, d_hidden, d_h1, d_h1_low, block_out = ([], [], [], [], [])
    gain_mlp_sum = jnp.zeros((width,), f32)
    for i in seqs:
        hidden = mm(n2[i], w_up_full)
        d_active = mm(cot[i], w_down_t)
        erf = lax.erf(hidden * 0.5**0.5)
        cdf = 0.5 + 0.5 * erf
        active.append((hidden * cdf).astype(bf16))
        slope = cdf + hidden * jnp.exp(-0.5 * hidden * hidden) * (0.5 / math.pi) ** 0.5
        d_hidden.append((d_active * slope).astype(bf16))
        d_n2_send = mm_rt(d_hidden[i][half:], w_up_full).astype(bf16)
        d_n2_keep = mm_rt(d_hidden[i][:half], w_up_full).astype(bf16)
        d_n2 = sum_chips(d_n2_keep.astype(f32) + exchange_core(d_n2_send).astype(f32))
        gain_mlp_sum = gain_mlp_sum + jnp.sum(d_n2 * unit1[i], axis=0)
        d_h1.append(cot[i][:half].astype(f32) + norm_back(unit1[i], inv1[i], mlp_g, d_n2))
        low = d_h1[i].astype(bf16)
        d_h1_low.append(jnp.concatenate([low, exchange_core(low)], axis=0))
        term = mm_rt(active[i], w_down_t)
        term = jnp.concatenate([term[:half] + h1[i] * (1.0 / chips), term[half:]], axis=0)
        block_out.append(to_features(term.astype(bf16), n_tensor).astype(bf16))
    cot_all = jnp.concatenate(cot, axis=0)
    grad2 = jnp.concatenate(
        [
            mm_lt(jnp.concatenate(n2, axis=0), jnp.concatenate(d_hidden, axis=0)).astype(bf16),
            mm_lt(cot_all, jnp.concatenate(active, axis=0)).astype(bf16),
        ],
        axis=1,
    )
    share2 = lax.psum_scatter(grad2, "dp", scatter_dimension=0, tiled=True).astype(f32)
    d_qkv, input_grad, seq_sums = ([], [], [])
    gain_attn_sum = jnp.zeros((width,), f32)
    for i in seqs:
        d_mixed = mm(d_h1_low[i], w1[:, 3 * shard :]).astype(bf16)
        parts = attend_back(
            query[i],
            key[i],
            value[i],
            same[i],
            scale,
            lse[i],
            d_mixed.reshape(seq_len, heads_dev, head_size),
        )
        d_qkv.append(
            jnp.concatenate([p.reshape(seq_len, shard).astype(bf16) for p in parts], axis=1)
        )
        d_n1 = mm_rt(d_qkv[i], w1[:, : 3 * shard])
        gain_attn_sum = gain_attn_sum + jnp.sum(d_n1 * unit0[i], axis=0)
        term = norm_back(unit0[i], inv0[i], attn_g, d_n1)
        term = jnp.concatenate([term[:half] + d_h1[i] * (1.0 / chips), term[half:]], axis=0)
        seq_sums.append(jnp.sum(term, axis=0))
        input_grad.append(to_features(term.astype(bf16), n_tensor))
    grad1 = jnp.concatenate(
        [
            mm_lt(jnp.concatenate(n1, axis=0), jnp.concatenate(d_qkv, axis=0)).astype(bf16),
            mm_lt(jnp.concatenate(d_h1_low, axis=0), jnp.concatenate(mixed, axis=0)).astype(bf16),
        ],
        axis=1,
    )
    share1 = ring.scatter(grad1)
    sums = jnp.zeros((n_seqs, width), f32)
    sums = lax.dynamic_update_slice_in_dim(sums, jnp.stack(seq_sums), me_dp * seqs_dev, 0)
    sums = jnp.concatenate([sums, gain_attn_sum[None], gain_mlp_sum[None] * (1.0 / chips)], axis=0)
    sums = lax.psum(sums, ("dp", "tensor"))
    rows = width // n_dp
    sums = lax.dynamic_slice_in_dim(sums, me_dp * rows, rows, 1)
    factor = float(n_seqs * seq_len) ** (-0.5)
    grad_time = (
        jnp.einsum("st,sd->td", temb, sums[:n_seqs], precision=lax.Precision.HIGHEST) * factor
    )

    def natural(value):
        return jnp.roll(value, core * half, axis=0)

    share1, share2 = (share1 * factor, share2 * factor)
    return (
        jnp.stack([natural(b) for b in block_out]),
        jnp.stack([natural(g) for g in input_grad]),
        jnp.stack([share1[:, c * shard : (c + 1) * shard] for c in range(3)]),
        share1[:, 3 * shard :].T,
        share2[:, :hidden_dev],
        share2[:, hidden_dev:].T,
        grad_time,
        sums[n_seqs] * factor,
        sums[n_seqs + 1] * factor,
    )


def solution(mesh):
    in_specs = (
        P("dp", None, None),
        P("dp", None),
        P("dp", None),
        P("dp"),
        P(None, "dp", "tensor"),
        P("tensor", "dp"),
        P("dp", "tensor"),
        P("tensor", "dp"),
        P(None, "dp"),
        P("dp"),
        P("dp"),
        P("dp", None, None),
    )
    out_specs = (
        P("dp", None, "tensor"),
        P("dp", None, "tensor"),
        P(None, "dp", "tensor"),
        P("tensor", "dp"),
        P("dp", "tensor"),
        P("tensor", "dp"),
        P(None, "dp"),
        P("dp"),
        P("dp"),
    )
    return jax.shard_map(shards, mesh=mesh, in_specs=in_specs, out_specs=out_specs, check_vma=False)
```

profile of v0, /device:TPU:0, one launch (start us, length us, event | category | flops | bytes accessed | tf_op | source)
XLA Modules:
  0.0 683.9 jit_solution(16655282718602888327)
XLA Ops:
  9.1 3.0 collective-permute-start
  14.9 12.1 %all-reduce = s32[16]{0:T(128)S(1)} all-reduce(s32[16]{0:T(128)S(1)} %dynamic-update-slice), channel_id=1, replica_groups=mesh['dp'=8,'tensor'=4] {'dp'}, use_global_device_ids=true, to_apply=%add | all-reduce | flops 16 | bytes 128
  28.4 31.2 %all_gather.10 = f32[18,1024]{1,0:T(8,128)S(1)} all-gather(f32[18,128]{1,0:T(8,128)S(1)} %pad_maximum_fusion.10), channel_id=1, replica_groups=mesh['dp'=8,'tensor'=4] {'dp'}, dimensions={1}, use_global_device_ids=true | all-gather | bytes 82944 | tf_op jit(solution)/shard_map/all_gather | solution.py:191
  59.7 4.7 slice_bitcast_fusion.3
  64.4 16.2 %multiply_sine_fusion.1 = (f32[1024,512]{1,0:T(8,128)S(1)}, f32[1024,512]{1,0:T(8,128)S(1)}, f32[1024,512]{1,0:T(8,128)}, f32[1024,512]{1,0:T(8,128)}) fusion(f32[512]{0:T(512)S(1)} %multiply_exponential_fusion, f32[1024]{0:T(1024)S(1)} %get-tuple-element.168, f32[1024]{0:T(1024)S(1)} %get-tuple-element.166), kind=kLoop, calls=%fused_computation.119 | loop fusion | flops 1048576 | bytes 8398848 | tf_op jit(solution)/shard_map/sin | solution.py:19
  106.7 2.3 collective-permute-done.5
  111.0 4.9 collective-permute-done.6
  118.0 7.5 %fusion.238 = (f32[4,1024]{1,0:T(4,128)S(1)}, f32[4,1024,1024]{1,2,0:T(8,128)}) fusion(bf16[1024,4,64]{0,2,1:T(8,128)(2,1)S(1)} %bitcast.178, bf16[1024,4,64]{0,2,1:T(8,128)(2,1)S(1)} %bitcast.176, pred[1024,1024]{0,1:T(8,128)(4,1)S(1)} %broadcast_compare_fusion.1), kind=kOutput, calls=%fused_computation.439 | convolution fusion | flops 549449728 | bytes 18890752 | tf_op jit(solution)/shard_map/qhe,khe->hqk/dot_general | solution.py:48
  125.5 8.0 %fusion = f32[4,1024]{1,0:T(4,128)S(1)} fusion(f32[4,1024,1024]{1,2,0:T(8,128)} %get-tuple-element.152, f32[4,1024]{1,0:T(4,128)S(1)} %get-tuple-element.151), kind=kLoop, calls=%fused_computation.12 | loop fusion | flops 8384512 | bytes 16809984 | tf_op jit(solution)/shard_map/reduce_sum | solution.py:52
  133.5 7.6 %fusion.144 = bf16[4,64,1024]{2,1,0:T(8,128)(2,1)S(1)} fusion(bf16[1024,4,64]{0,2,1:T(8,128)(2,1)S(1)} %bitcast.188, f32[4,1024,1024]{1,2,0:T(8,128)} %get-tuple-element.152, f32[4,1024]{1,0:T(4,128)S(1)} %fusion, f32[4,1024]{1,0:T(4,128)S(1)} %get-tuple-element.151), kind=kOutput, calls=%fused_computation.250 | convolution fusion | flops 549715968 | bytes 17858560 | tf_op jit(solution)/shard_map/hqk,khe->qhe/dot_general | solution.py:54
  146.3 23.7 %collective-permute-done.8 = bf16[512,1024]{1,0:T(8,128)(2,1)S(1)} collective-permute-done((bf16[512,1024]{1,0:T(8,128)(2,1)S(1)}, bf16[512,1024]{1,0:T(8,128)(2,1)S(1)}, u32[]{:S(2)}, u32[]{:S(2)}) %collective-permute-start.8) | collective-permute-done | bytes 1048608 | tf_op jit(solution)/shard_map/ppermute | solution.py:133
  174.7 4.1 fusion.68
  178.9 4.7 multiply_convert_fusion.4
  183.6 3.7 fusion.17
  188.8 2.6 collective-permute-done.17
  194.3 2.9 fusion.225
  197.2 2.4 fusion.122
  203.1 2.9 copy.144
  206.0 12.1 %collective-permute-done.18 = bf16[512,1024]{1,0:T(8,128)(2,1)} collective-permute-done((bf16[512,1024]{1,0:T(8,128)(2,1)S(1)}, bf16[512,1024]{1,0:T(8,128)(2,1)}, u32[]{:S(2)}, u32[]{:S(2)}) %collective-permute-start.18) | collective-permute-done | bytes 1048608 | tf_op jit(solution)/shard_map/ppermute | solution.py:133
  218.0 2.7 multiply_reduce_fusion.11
  220.8 3.5 fusion.219
  227.0 2.6 fusion.133
  229.7 9.4 %fusion.124 = bf16[4,64,1024]{2,1,0:T(8,128)(2,1)} fusion(bf16[1024,4,64]{0,2,1:T(8,128)(2,1)S(1)} %bitcast.182, f32[4,1024,1024]{1,2,0:T(8,128)} %get-tuple-element.152, f32[4,1024]{1,0:T(4,128)S(1)} %log_add_fusion.1), kind=kOutput, calls=%fused_computation.240 | convolution fusion | flops 545521664 | bytes 17842176 | tf_op jit(solution)/shard_map/hqk,qhe->khe/dot_general | solution.py:63
  239.1 7.6 %multiply_reduce_fusion.1 = (f32[4,1024]{1,0:T(4,128)S(1)}, f32[4,1024,1024]{1,2,0:T(8,128)}) fusion(f32[4,1024,1024]{1,2,0:T(8,128)S(1)} %bitcast.171, f32[4,1024]{1,0:T(4,128)S(1)} %log_add_fusion.1, bf16[1024,4,64]{0,2,1:T(8,128)(2,1)S(1)} %bitcast.183, bf16[1024,4,64]{0,2,1:T(8,128)(2,1)S(1)} %bitcast.189), kind=kOutput, calls=%fused_computation.4 | convolution fusion | flops 549449728 | bytes 34635776 | tf_op jit(solution)/shard_map/qhe,khe->hqk/dot_general | solution.py:62
  246.7 8.3 %multiply_convert_fusion.1 = bf16[4,1024,1024]{1,2,0:T(8,128)(2,1)S(1)} fusion(f32[4,1024,1024]{1,2,0:T(8,128)} %get-tuple-element.156, f32[4,1024,1024]{1,2,0:T(8,128)S(1)} %bitcast.171, f32[4,1024]{1,0:T(4,128)S(1)} %get-tuple-element.155, f32[4,1024]{1,0:T(4,128)S(1)} %log_add_fusion.1), kind=kLoop, calls=%fused_computation.3 | loop fusion | flops 16777216 | bytes 41975808 | tf_op jit(solution)/shard_map/convert_element_type | solution.py:65
  255.0 2.7 fusion.137
  261.0 3.5 multiply_reduce_fusion.3
  264.5 3.5 subtract_multiply_fusion.1
  270.1 7.5 %fusion.239 = (f32[4,1024]{1,0:T(4,128)S(1)}, f32[4,1024,1024]{1,2,0:T(8,128)}) fusion(bf16[1024,4,64]{0,2,1:T(8,128)(2,1)S(1)} %bitcast.174, bf16[1024,4,64]{0,2,1:T(8,128)(2,1)S(1)} %bitcast.172, pred[1024,1024]{0,1:T(8,128)(4,1)S(1)} %broadcast_compare_fusion), kind=kOutput, calls=%fused_computation.440 | convolution fusion | flops 549449728 | bytes 18890752 | tf_op jit(solution)/shard_map/qhe,khe->hqk/dot_general | solution.py:48
  277.5 8.0 %fusion.1 = f32[4,1024]{1,0:T(4,128)S(1)} fusion(f32[4,1024,1024]{1,2,0:T(8,128)} %get-tuple-element.159, f32[4,1024]{1,0:T(4,128)S(1)} %get-tuple-element.158), kind=kLoop, calls=%fused_computation.13 | loop fusion | flops 8384512 | bytes 16809984 | tf_op jit(solution)/shard_map/reduce_sum | solution.py:52
  285.6 7.7 %fusion.143 = bf16[4,64,1024]{2,1,0:T(8,128)(2,1)S(1)} fusion(bf16[1024,4,64]{0,2,1:T(8,128)(2,1)S(1)} %bitcast.186, f32[4,1024,1024]{1,2,0:T(8,128)} %get-tuple-element.159, f32[4,1024]{1,0:T(4,128)S(1)} %fusion.1, f32[4,1024]{1,0:T(4,128)S(1)} %get-tuple-element.158), kind=kOutput, calls=%fused_computation.249 | convolution fusion | flops 549715968 | bytes 17858560 | tf_op jit(solution)/shard_map/hqk,khe->qhe/dot_general | solution.py:54
  298.5 23.7 %collective-permute-done.13 = bf16[512,1024]{1,0:T(8,128)(2,1)S(1)} collective-permute-done((bf16[512,1024]{1,0:T(8,128)(2,1)S(1)}, bf16[512,1024]{1,0:T(8,128)(2,1)S(1)}, u32[]{:S(2)}, u32[]{:S(2)}) %collective-permute-start.13) | collective-permute-done | bytes 1048608 | tf_op jit(solution)/shard_map/ppermute | solution.py:133
  324.3 4.7 fusion.67
  329.0 2.7 slice.402
  334.0 2.6 concatenate.137
  340.2 5.5 multiply_convert_fusion.2
  345.7 3.7 fusion.23
  356.2 2.8 concatenate.150
  359.0 2.6 concatenate.149
  366.5 3.9 add_convert_fusion
  371.9 2.4 fusion.120
  377.9 2.9 copy.145
  380.8 9.4 %fusion.89 = bf16[1024,1024]{0,1:T(8,128)(2,1)} fusion(bf16[1024,1024]{1,0:T(8,128)(2,1)} %get-tuple-element.160, bf16[1024,1024]{1,0:T(8,128)(2,1)} %copy-done.109, bf16[1024,1024]{1,0:T(8,128)(2,1)} %fusion.67, bf16[1024,1024]{1,0:T(8,128)(2,1)} %fusion.68), kind=kOutput, calls=%fused_computation.203 | convolution fusion | flops 4312793088 | bytes 10485760 | tf_op jit(solution)/shard_map/ki,kj->ij/dot_general | solution.py:80
  390.2 5.9 collective-permute-done.23
  396.1 2.5 multiply_reduce_fusion.10
  398.6 4.4 fusion.220
  403.2 9.2 %fusion.94 = bf16[1024,1024]{0,1:T(8,128)(2,1)} fusion(bf16[1024,1024]{1,0:T(8,128)(2,1)} %copy-done.108, bf16[1024,1024]{1,0:T(8,128)(2,1)} %copy-done.107, bf16[512,1024]{1,0:T(8,128)(2,1)} %collective-permute-done.14, bf16[512,1024]{1,0:T(8,128)(2,1)} %multiply_convert_fusion.6, bf16[512,1024]{1,0:T(8,128)(2,1)} %collective-permute-done.9, ...), kind=kOutput, calls=%fused_computation.204 | convolution fusion | flops 4321181696 | bytes 10485760 | tf_op jit(solution)/shard_map/ki,kj->ij/dot_general | solution.py:80
  415.5 3.6 fusion.127
  419.0 10.5 %multiply_reduce_fusion = (f32[4,1024]{1,0:T(4,128)S(1)}, f32[4,1024,1024]{1,2,0:T(8,128)}) fusion(f32[4,1024,1024]{1,2,0:T(8,128)S(1)} %bitcast.169, f32[4,1024]{1,0:T(4,128)S(1)} %log_add_fusion, bf16[1024,4,64]{0,2,1:T(8,128)(2,1)} %bitcast.185, bf16[1024,4,64]{0,2,1:T(8,128)(2,1)} %bitcast.187), kind=kOutput, calls=%fused_computation.1 | convolution fusion | flops 549449728 | bytes 34635776 | tf_op jit(solution)/shard_map/qhe,khe->hqk/dot_general | solution.py:62
  429.6 8.0 %multiply_convert_fusion = bf16[4,1024,1024]{1,2,0:T(8,128)(2,1)S(1)} fusion(f32[4,1024,1024]{1,2,0:T(8,128)} %get-tuple-element.163, f32[4,1024,1024]{1,2,0:T(8,128)S(1)} %bitcast.169, f32[4,1024]{1,0:T(4,128)S(1)} %get-tuple-element.162, f32[4,1024]{1,0:T(4,128)S(1)} %log_add_fusion), kind=kLoop, calls=%fused_computation | loop fusion | flops 16777216 | bytes 41975808 | tf_op jit(solution)/shard_map/convert_element_type | solution.py:65
  437.7 2.7 fusion.139
  442.8 2.8 multiply_reduce_fusion.2
  450.5 4.1 pad_maximum_fusion
  454.6 6.7 copy.139
  483.2 7.7 %collective-permute-done.21 = bf16[1024,1,256]{2,0,1:T(8,128)(2,1)} collective-permute-done((bf16[1024,1,256]{2,0,1:T(8,128)(2,1)}, bf16[1024,1,256]{2,0,1:T(8,128)(2,1)}, u32[]{:S(2)}, u32[]{:S(2)}) %collective-permute-start.21) | collective-permute-done | bytes 524320 | tf_op jit(solution)/shard_map/ppermute | solution.py:133
  493.6 2.8 slice.403
  499.4 2.9 fusion.140
  503.0 3.4 fusion.99
  513.0 2.7 collective-permute-done.27
  520.4 49.7 %all-reduce.3.cloned.1.call-done = f32[18,1024]{1,0:T(8,128)} async-done(((f32[18,1024]{1,0:T(8,128)}), f32[18,1024]{1,0:T(8,128)}) %all-reduce.3.cloned.1.call-update) | async-done | bytes 73744 | tf_op jit(solution)/shard_map/psum | solution.py:312
  573.0 3.3 collective-permute-start.29
  585.8 14.7 %collective-permute-done.32 = bf16[128,1024]{0,1:T(8,128)(2,1)S(1)} collective-permute-done((bf16[128,1024]{0,1:T(8,128)(2,1)S(1)}, bf16[128,1024]{0,1:T(8,128)(2,1)S(1)}, u32[]{:S(2)}, u32[]{:S(2)}) %collective-permute-start.32) | collective-permute-done | bytes 262176 | tf_op jit(solution)/shard_map/ppermute | solution.py:124
  604.5 16.3 %collective-permute-done.33 = bf16[128,1024]{0,1:T(8,128)(2,1)S(1)} collective-permute-done((bf16[128,1024]{0,1:T(8,128)(2,1)S(1)}, bf16[128,1024]{0,1:T(8,128)(2,1)S(1)}, u32[]{:S(2)}, u32[]{:S(2)}) %collective-permute-start.33) | collective-permute-done | bytes 262176 | tf_op jit(solution)/shard_map/ppermute | solution.py:124
  625.9 47.9 %reduce-scatter.4.cloned.1.call-done = bf16[128,2048]{1,0:T(8,128)(2,1)} async-done(((bf16[1024,2048]{1,0:T(8,128)(2,1)}), bf16[128,2048]{1,0:T(8,128)(2,1)}) %reduce-scatter.4.cloned.1.call-update) | async-done | bytes 524304
  (455 shorter events, 151.7 us)
Async XLA Ops:
  7.2 20.7 %copy-start = (bf16[256,128]{1,0:T(8,128)(2,1)S(1)}, bf16[256,128]{1,0:T(8,128)(2,1)}, u32[]{:S(2)}) copy-start(bf16[256,128]{1,0:T(8,128)(2,1)} %param.30) | copy-start | bytes 196612
  7.2 171.6 %all-gather.2.cloned.1.call-start = ((), (), s32[]{:S(2)}) async-start(), calls=%async_computation.1 | async-start | bytes 4718592 | tf_op jit(solution)/shard_map/all_gather | solution.py:184
  8.7 18.3 %copy-start.96 = (s32[2,8]{1,0:T(2,128)S(1)}, s32[2,8]{1,0:T(2,128)}, u32[]{:S(2)}) copy-start(s32[2,8]{1,0:T(2,128)} %param.24) | copy-start | bytes 196
  8.7 18.3 %copy-start.94 = (s32[2,1024]{1,0:T(2,128)S(1)}, s32[2,1024]{1,0:T(2,128)}, u32[]{:S(2)}) copy-start(s32[2,1024]{1,0:T(2,128)} %param.23) | copy-start | bytes 24580
  8.7 19.0 %copy-start.97 = (bf16[128]{0:T(256)(128)(2,1)S(1)}, bf16[128]{0:T(256)(128)(2,1)}, u32[]{:S(2)}) copy-start(bf16[128]{0:T(256)(128)(2,1)} %param.32) | copy-start | bytes 772
  8.7 19.0 %copy-start.98 = (bf16[128]{0:T(256)(128)(2,1)S(1)}, bf16[128]{0:T(256)(128)(2,1)}, u32[]{:S(2)}) copy-start(bf16[128]{0:T(256)(128)(2,1)} %param.31) | copy-start | bytes 772
  9.1 77.5 %collective-permute-start = (bf16[128,1024]{0,1:T(8,128)(2,1)S(1)}, bf16[128,1024]{0,1:T(8,128)(2,1)}, u32[]{:S(2)}, u32[]{:S(2)}) collective-permute-start(bf16[128,1024]{0,1:T(8,128)(2,1)S(1)} %get-tuple-element.117), channel_id=1, source_target_pairs={{8,0},{16,8},{24,16},{28,24},{20,28},{12,20},{4,12},{0,4},{9,1},{1... | collective-permute-start | bytes 786440 | tf_op jit(solution)/shard_map/ppermute | solution.py:106
  12.1 74.6 %collective-permute-start.1 = (bf16[128,1024]{0,1:T(8,128)(2,1)S(1)}, bf16[128,1024]{0,1:T(8,128)(2,1)S(1)}, u32[]{:S(2)}, u32[]{:S(2)}) collective-permute-start(bf16[128,1024]{0,1:T(8,128)(2,1)S(1)} %get-tuple-element.117), channel_id=1, source_target_pairs={{0,8},{8,16},{16,24},{24,28},{28,20},{20,12},{12,4},{4,0},{1,9},{9... | collective-permute-start | bytes 786440 | tf_op jit(solution)/shard_map/ppermute | solution.py:104
  13.3 556.8 %all-reduce.3.cloned.1.call-start = ((), (), s32[]{:S(2)}) async-start(), calls=%async_computation.2 | async-start | bytes 196608 | tf_op jit(solution)/shard_map/psum | solution.py:312
  64.4 16.3 %copy-start.25 = (bf16[1024,1024]{1,0:T(8,128)(2,1)S(1)}, bf16[1024,1024]{1,0:T(8,128)(2,1)}, u32[]{:S(2)}) copy-start(bf16[1024,1024]{1,0:T(8,128)(2,1)} %get-tuple-element.85) | copy-start | bytes 6291460
  84.7 12.5 %copy-start.92 = (s32[8]{0:T(128)S(1)}, s32[8]{0:T(128)}, u32[]{:S(2)}) copy-start(s32[8]{0:T(128)} %constant.326.clone) | copy-start | bytes 100
  86.6 17.2 %collective-permute-start.2 = (bf16[128,1024]{0,1:T(8,128)(2,1)}, bf16[128,1024]{0,1:T(8,128)(2,1)}, u32[]{:S(2)}, u32[]{:S(2)}) collective-permute-start(bf16[128,1024]{0,1:T(8,128)(2,1)} %collective-permute-done), channel_id=1, source_target_pairs={{8,0},{16,8},{24,16},{28,24},{20,28},{12,20},{4,12},{0,4},{9,1},{1... | collective-permute-start | bytes 786440 | tf_op jit(solution)/shard_map/ppermute | solution.py:106
  86.6 15.7 %collective-permute-start.3 = (bf16[128,1024]{0,1:T(8,128)(2,1)S(1)}, bf16[128,1024]{0,1:T(8,128)(2,1)}, u32[]{:S(2)}, u32[]{:S(2)}) collective-permute-start(bf16[128,1024]{0,1:T(8,128)(2,1)S(1)} %collective-permute-done.1), channel_id=1, source_target_pairs={{0,8},{8,16},{16,24},{24,28},{28,20},{20,12},{12,4},{4,0},{1,9},{9... | collective-permute-start | bytes 786440 | tf_op jit(solution)/shard_map/ppermute | solution.py:104
  102.4 13.6 %copy-start.59 = (bf16[1024,1024]{1,0:T(8,128)(2,1)S(1)}, bf16[1024,1024]{1,0:T(8,128)(2,1)}, u32[]{:S(2)}) copy-start(bf16[1024,1024]{1,0:T(8,128)(2,1)} %multiply_convert_fusion.5) | copy-start | bytes 6291460
  102.4 6.6 collective-permute-start.5
  103.8 6.9 %collective-permute-start.4 = (bf16[128,1024]{0,1:T(8,128)(2,1)}, bf16[128,1024]{0,1:T(8,128)(2,1)S(1)}, u32[]{:S(2)}, u32[]{:S(2)}) collective-permute-start(bf16[128,1024]{0,1:T(8,128)(2,1)} %collective-permute-done.2), channel_id=1, source_target_pairs={{8,0},{16,8},{24,16},{28,24},{20,28},{12,20},{4,12},{0,4},{9,1},{1... | collective-permute-start | bytes 786440 | tf_op jit(solution)/shard_map/ppermute | solution.py:106
  109.0 6.9 %collective-permute-start.6 = (bf16[128,1024]{0,1:T(8,128)(2,1)S(1)}, bf16[128,1024]{0,1:T(8,128)(2,1)S(1)}, u32[]{:S(2)}, u32[]{:S(2)}) collective-permute-start(bf16[128,1024]{0,1:T(8,128)(2,1)S(1)} %collective-permute-done.5), channel_id=1, source_target_pairs={{0,8},{8,16},{16,24},{24,28},{28,20},{20,12},{12,4},{4,0},{1,9},{9... | collective-permute-start | bytes 786440 | tf_op jit(solution)/shard_map/ppermute | solution.py:104
  116.0 25.7 %copy-start.14 = (bf16[1024,1024]{0,1:T(8,128)(2,1)}, bf16[1024,1024]{0,1:T(8,128)(2,1)S(1)}, u32[]{:S(2)}) copy-start(bf16[1024,1024]{0,1:T(8,128)(2,1)S(1)} %constant_dynamic-update-slice_fusion.1) | copy-start | bytes 6291460
  118.0 15.5 %copy-start.57 = (bf16[1024,256]{0,1:T(8,128)(2,1)}, bf16[1024,256]{0,1:T(8,128)(2,1)S(1)}, u32[]{:S(2)}) copy-start(bf16[1024,256]{0,1:T(8,128)(2,1)S(1)} %get-tuple-element.95) | copy-start | bytes 1572868
  141.6 2.7 collective-permute-start.7
  141.7 28.3 %copy-start.6 = (f32[1024,1024]{1,0:T(8,128)S(1)}, f32[1024,1024]{1,0:T(8,128)}, u32[]{:S(2)}) copy-start(f32[1024,1024]{1,0:T(8,128)} %copy-done.5) | copy-start | bytes 12582916
  144.7 25.3 %collective-permute-start.8 = (bf16[512,1024]{1,0:T(8,128)(2,1)S(1)}, bf16[512,1024]{1,0:T(8,128)(2,1)S(1)}, u32[]{:S(2)}, u32[]{:S(2)}) collective-permute-start(bf16[512,1024]{1,0:T(8,128)(2,1)S(1)} %add_convert_fusion.5), channel_id=1, source_target_pairs={{0,2},{1,3},{2,0},{3,1},{4,6},{5,7},{6,4},{7,5},{8,10},{9,11},{10,... | collective-permute-start | bytes 3145736 | tf_op jit(solution)/shard_map/ppermute | solution.py:133
  171.1 7.7 %collective-permute-start.9 = (bf16[512,1024]{1,0:T(8,128)(2,1)S(1)}, bf16[512,1024]{1,0:T(8,128)(2,1)}, u32[]{:S(2)}, u32[]{:S(2)}) collective-permute-start(bf16[512,1024]{1,0:T(8,128)(2,1)S(1)} %multiply_convert_fusion.7), channel_id=1, source_target_pairs={{0,1},{1,0},{2,3},{3,2},{4,5},{5,4},{6,7},{7,6},{8,9},{9,8},{10,11... | collective-permute-start | bytes 3145736 | tf_op jit(solution)/shard_map/ppermute | solution.py:133
  183.6 13.5 %copy-start.109 = (bf16[1024,1024]{1,0:T(8,128)(2,1)}, bf16[1024,1024]{1,0:T(8,128)(2,1)S(1)}, u32[]{:S(2)}) copy-start(bf16[1024,1024]{1,0:T(8,128)(2,1)S(1)} %get-tuple-element.153) | copy-start | bytes 6291460
  188.7 2.7 collective-permute-start.17
  192.7 25.4 %collective-permute-start.18 = (bf16[512,1024]{1,0:T(8,128)(2,1)S(1)}, bf16[512,1024]{1,0:T(8,128)(2,1)}, u32[]{:S(2)}, u32[]{:S(2)}) collective-permute-start(bf16[512,1024]{1,0:T(8,128)(2,1)S(1)} %add_convert_fusion.1), channel_id=1, source_target_pairs={{0,2},{1,3},{2,0},{3,1},{4,6},{5,7},{6,4},{7,5},{8,10},{9,11},{10,... | collective-permute-start | bytes 3145736 | tf_op jit(solution)/shard_map/ppermute | solution.py:133
  206.0 14.8 %copy-start.19 = (f32[512,1024]{1,0:T(8,128)S(1)}, f32[512,1024]{1,0:T(8,128)}, u32[]{:S(2)}) copy-start(f32[512,1024]{1,0:T(8,128)} %copy.144) | copy-start | bytes 6291460
  206.0 14.8 %copy-start.40 = (bf16[1024,1024]{1,0:T(8,128)(2,1)S(1)}, bf16[1024,1024]{1,0:T(8,128)(2,1)}, u32[]{:S(2)}) copy-start(bf16[1024,1024]{1,0:T(8,128)(2,1)} %fusion.68) | copy-start | bytes 6291460
  220.8 18.3 %slice-start.4 = ((s8[16777216]{0:T(1024)(128)(4,1)}), s8[4194304]{0:T(1024)(128)(4,1)S(1)}, s32[]{:S(2)}) async-start(s8[16777216]{0:T(1024)(128)(4,1)} %bitcast.170), calls=%async_computation.8 | async-start | bytes 8388608
  220.8 18.3 %slice-start.5 = ((s8[16777216]{0:T(1024)(128)(4,1)}), s8[4194304]{0:T(1024)(128)(4,1)S(1)}, s32[]{:S(2)}) async-start(s8[16777216]{0:T(1024)(128)(4,1)} %bitcast.170), calls=%async_computation.9 | async-start | bytes 8388608
  224.4 2.7 collective-permute-start.19
  225.6 13.4 %slice-start.6 = ((s8[16777216]{0:T(1024)(128)(4,1)}), s8[4194304]{0:T(1024)(128)(4,1)S(1)}, s32[]{:S(2)}) async-start(s8[16777216]{0:T(1024)(128)(4,1)} %bitcast.170), calls=%async_computation.10 | async-start | bytes 8388608
  229.6 9.4 %slice-start.7 = ((s8[16777216]{0:T(1024)(128)(4,1)}), s8[4194304]{0:T(1024)(128)(4,1)S(1)}, s32[]{:S(2)}) async-start(s8[16777216]{0:T(1024)(128)(4,1)} %bitcast.170), calls=%async_computation.11 | async-start | bytes 8388608
  270.1 15.5 %copy-start.56 = (bf16[1024,256]{0,1:T(8,128)(2,1)}, bf16[1024,256]{0,1:T(8,128)(2,1)S(1)}, u32[]{:S(2)}) copy-start(bf16[1024,256]{0,1:T(8,128)(2,1)S(1)} %get-tuple-element.98) | copy-start | bytes 1572868
  293.8 2.7 collective-permute-start.12
  296.9 25.3 %collective-permute-start.13 = (bf16[512,1024]{1,0:T(8,128)(2,1)S(1)}, bf16[512,1024]{1,0:T(8,128)(2,1)S(1)}, u32[]{:S(2)}, u32[]{:S(2)}) collective-permute-start(bf16[512,1024]{1,0:T(8,128)(2,1)S(1)} %add_convert_fusion.3), channel_id=1, source_target_pairs={{0,2},{1,3},{2,0},{3,1},{4,6},{5,7},{6,4},{7,5},{8,10},{9,11},{10,... | collective-permute-start | bytes 3145736 | tf_op jit(solution)/shard_map/ppermute | solution.py:133
  324.3 15.6 %collective-permute-start.14 = (bf16[512,1024]{1,0:T(8,128)(2,1)}, bf16[512,1024]{1,0:T(8,128)(2,1)}, u32[]{:S(2)}, u32[]{:S(2)}) collective-permute-start(bf16[512,1024]{1,0:T(8,128)(2,1)} %multiply_convert_fusion.6), channel_id=1, source_target_pairs={{0,1},{1,0},{2,3},{3,2},{4,5},{5,4},{6,7},{7,6},{8,9},{9,8},{10,11... | collective-permute-start | bytes 3145736 | tf_op jit(solution)/shard_map/ppermute | solution.py:133
  339.5 121.9 %collective-permute-start.10 = (bf16[1024,2,256]{2,0,1:T(8,128)(2,1)}, bf16[1024,2,256]{2,0,1:T(8,128)(2,1)}, u32[]{:S(2)}, u32[]{:S(2)}) collective-permute-start(bf16[1024,2,256]{2,0,1:T(8,128)(2,1)} %fusion.154), channel_id=1, source_target_pairs={{0,1},{1,0},{2,3},{3,2},{4,5},{5,4},{6,7},{7,6},{8,9},{9,8},{10,11... | collective-permute-start | bytes 3145736 | tf_op jit(solution)/shard_map/ppermute | solution.py:133
  351.7 14.5 %collective-permute-start.22 = (bf16[512,1024]{1,0:T(8,128)(2,1)}, bf16[512,1024]{1,0:T(8,128)(2,1)}, u32[]{:S(2)}, u32[]{:S(2)}) collective-permute-start(bf16[512,1024]{1,0:T(8,128)(2,1)} %convolution_convert_fusion.2), channel_id=1, source_target_pairs={{0,1},{1,0},{2,3},{3,2},{4,5},{5,4},{6,7},{7,6},{8,9},{9,8},{10,11... | collective-permute-start | bytes 3145736 | tf_op jit(solution)/shard_map/ppermute | solution.py:133
  365.6 100.3 %collective-permute-start.20 = (bf16[1024,2,256]{2,0,1:T(8,128)(2,1)}, bf16[1024,2,256]{2,0,1:T(8,128)(2,1)}, u32[]{:S(2)}, u32[]{:S(2)}) collective-permute-start(bf16[1024,2,256]{2,0,1:T(8,128)(2,1)} %dynamic-slice_bitcast_fusion.1), channel_id=1, source_target_pairs={{0,1},{1,0},{2,3},{3,2},{4,5},{5,4},{6,7},{7,6},{8,9},{9,8},{10,11... | collective-permute-start | bytes 3145736 | tf_op jit(solution)/shard_map/ppermute | solution.py:133
  370.4 25.7 %collective-permute-start.23 = (bf16[512,1024]{1,0:T(8,128)(2,1)}, bf16[512,1024]{1,0:T(8,128)(2,1)}, u32[]{:S(2)}, u32[]{:S(2)}) collective-permute-start(bf16[512,1024]{1,0:T(8,128)(2,1)} %add_convert_fusion), channel_id=1, source_target_pairs={{0,2},{1,3},{2,0},{3,1},{4,6},{5,7},{6,4},{7,5},{8,10},{9,11},{10,... | collective-permute-start | bytes 3145736 | tf_op jit(solution)/shard_map/ppermute | solution.py:133
  398.6 16.9 %slice-start = ((s8[16777216]{0:T(1024)(128)(4,1)}), s8[4194304]{0:T(1024)(128)(4,1)S(1)}, s32[]{:S(2)}) async-start(s8[16777216]{0:T(1024)(128)(4,1)} %bitcast.168), calls=%async_computation.4 | async-start | bytes 8388608
  403.0 12.4 %slice-start.1 = ((s8[16777216]{0:T(1024)(128)(4,1)}), s8[4194304]{0:T(1024)(128)(4,1)S(1)}, s32[]{:S(2)}) async-start(s8[16777216]{0:T(1024)(128)(4,1)} %bitcast.168), calls=%async_computation.5 | async-start | bytes 8388608
  403.1 12.4 %slice-start.2 = ((s8[16777216]{0:T(1024)(128)(4,1)}), s8[4194304]{0:T(1024)(128)(4,1)S(1)}, s32[]{:S(2)}) async-start(s8[16777216]{0:T(1024)(128)(4,1)} %bitcast.168), calls=%async_computation.6 | async-start | bytes 8388608
  403.1 12.4 %slice-start.3 = ((s8[16777216]{0:T(1024)(128)(4,1)}), s8[4194304]{0:T(1024)(128)(4,1)S(1)}, s32[]{:S(2)}) async-start(s8[16777216]{0:T(1024)(128)(4,1)} %bitcast.168), calls=%async_computation.7 | async-start | bytes 8388608
  403.1 9.3 %collective-permute-start.24 = (bf16[512,1024]{1,0:T(8,128)(2,1)}, bf16[512,1024]{1,0:T(8,128)(2,1)}, u32[]{:S(2)}, u32[]{:S(2)}) collective-permute-start(bf16[512,1024]{1,0:T(8,128)(2,1)} %get-tuple-element.71), channel_id=1, source_target_pairs={{0,1},{1,0},{2,3},{3,2},{4,5},{5,4},{6,7},{7,6},{8,9},{9,8},{10,11... | collective-permute-start | bytes 3145736 | tf_op jit(solution)/shard_map/ppermute | solution.py:133
  450.2 223.6 %reduce-scatter.4.cloned.1.call-start = ((), (), s32[]{:S(2)}) async-start(), calls=%async_computation.3 | async-start | bytes 4718592
  464.4 15.1 %collective-permute-start.11 = (bf16[1024,1,256]{2,0,1:T(8,128)(2,1)}, bf16[1024,1,256]{2,0,1:T(8,128)(2,1)}, u32[]{:S(2)}, u32[]{:S(2)}) collective-permute-start(bf16[1024,1,256]{2,0,1:T(8,128)(2,1)} %dynamic-slice_convert_fusion.3), channel_id=1, source_target_pairs={{0,2},{1,3},{2,0},{3,1},{4,6},{5,7},{6,4},{7,5},{8,10},{9,11},{10,... | collective-permute-start | bytes 1572872 | tf_op jit(solution)/shard_map/ppermute | solution.py:133
  473.2 23.1 %collective-permute-start.15 = (bf16[1024,2,256]{2,0,1:T(8,128)(2,1)}, bf16[1024,2,256]{2,0,1:T(8,128)(2,1)S(1)}, u32[]{:S(2)}, u32[]{:S(2)}) collective-permute-start(bf16[1024,2,256]{2,0,1:T(8,128)(2,1)} %fusion.150), channel_id=1, source_target_pairs={{0,1},{1,0},{2,3},{3,2},{4,5},{5,4},{6,7},{7,6},{8,9},{9,8},{10,11... | collective-permute-start | bytes 3145736 | tf_op jit(solution)/shard_map/ppermute | solution.py:133
  476.0 15.0 %collective-permute-start.21 = (bf16[1024,1,256]{2,0,1:T(8,128)(2,1)}, bf16[1024,1,256]{2,0,1:T(8,128)(2,1)}, u32[]{:S(2)}, u32[]{:S(2)}) collective-permute-start(bf16[1024,1,256]{2,0,1:T(8,128)(2,1)} %dynamic-slice_convert_fusion.1), channel_id=1, source_target_pairs={{0,2},{1,3},{2,0},{3,1},{4,6},{5,7},{6,4},{7,5},{8,10},{9,11},{10,... | collective-permute-start | bytes 1572872 | tf_op jit(solution)/shard_map/ppermute | solution.py:133
  478.1 12.8 %copy-start.29 = (f32[1024,2,256]{2,0,1:T(8,128)S(1)}, f32[1024,2,256]{2,0,1:T(8,128)}, u32[]{:S(2)}) copy-start(f32[1024,2,256]{2,0,1:T(8,128)} %maximum_add_fusion.4) | copy-start | bytes 6291460
  497.7 80.0 %collective-permute-start.16 = (bf16[1024,1,256]{2,0,1:T(8,128)(2,1)}, bf16[1024,1,256]{2,0,1:T(8,128)(2,1)}, u32[]{:S(2)}, u32[]{:S(2)}) collective-permute-start(bf16[1024,1,256]{2,0,1:T(8,128)(2,1)} %dynamic-slice_convert_fusion.2), channel_id=1, source_target_pairs={{0,2},{1,3},{2,0},{3,1},{4,6},{5,7},{6,4},{7,5},{8,10},{9,11},{10,... | collective-permute-start | bytes 1572872 | tf_op jit(solution)/shard_map/ppermute | solution.py:133
  507.4 8.2 %collective-permute-start.27 = (bf16[128,1024]{0,1:T(8,128)(2,1)}, bf16[128,1024]{0,1:T(8,128)(2,1)}, u32[]{:S(2)}, u32[]{:S(2)}) collective-permute-start(bf16[128,1024]{0,1:T(8,128)(2,1)} %get-tuple-element.89), channel_id=1, source_target_pairs={{0,8},{8,16},{16,24},{24,28},{28,20},{20,12},{12,4},{4,0},{1,9},{9... | collective-permute-start | bytes 786440 | tf_op jit(solution)/shard_map/ppermute | solution.py:124
  507.7 71.2 %collective-permute-start.31 = (bf16[128,1024]{0,1:T(8,128)(2,1)}, bf16[128,1024]{0,1:T(8,128)(2,1)S(1)}, u32[]{:S(2)}, u32[]{:S(2)}) collective-permute-start(bf16[128,1024]{0,1:T(8,128)(2,1)} %get-tuple-element.90), channel_id=1, source_target_pairs={{8,0},{16,8},{24,16},{28,24},{20,28},{12,20},{4,12},{0,4},{9,1},{1... | collective-permute-start | bytes 786440 | tf_op jit(solution)/shard_map/ppermute | solution.py:124
  517.4 52.7 %copy-start.88 = (f32[16,128]{1,0:T(8,128)S(1)}, f32[16,128]{1,0:T(8,128)}, u32[]{:S(2)}) copy-start(f32[16,128]{1,0:T(8,128)} %copy-done.87) | copy-start | bytes 24580
  517.4 52.7 %copy-start.90 = (f32[16,128]{1,0:T(8,128)S(1)}, f32[16,128]{1,0:T(8,128)}, u32[]{:S(2)}) copy-start(f32[16,128]{1,0:T(8,128)} %copy-done.89) | copy-start | bytes 24580
  517.4 54.6 %collective-permute-start.28 = (bf16[128,1024]{0,1:T(8,128)(2,1)}, bf16[128,1024]{0,1:T(8,128)(2,1)}, u32[]{:S(2)}, u32[]{:S(2)}) collective-permute-start(bf16[128,1024]{0,1:T(8,128)(2,1)} %add_convert_fusion.12), channel_id=1, source_target_pairs={{0,8},{8,16},{16,24},{24,28},{28,20},{20,12},{12,4},{4,0},{1,9},{9... | collective-permute-start | bytes 786440 | tf_op jit(solution)/shard_map/ppermute | solution.py:124
  520.4 80.2 %collective-permute-start.25 = (bf16[1024,2,256]{2,0,1:T(8,128)(2,1)}, bf16[1024,2,256]{2,0,1:T(8,128)(2,1)S(1)}, u32[]{:S(2)}, u32[]{:S(2)}) collective-permute-start(bf16[1024,2,256]{2,0,1:T(8,128)(2,1)} %dynamic-slice_bitcast_fusion), channel_id=1, source_target_pairs={{0,1},{1,0},{2,3},{3,2},{4,5},{5,4},{6,7},{7,6},{8,9},{9,8},{10,11... | collective-permute-start | bytes 3145736 | tf_op jit(solution)/shard_map/ppermute | solution.py:133
  573.0 7.8 %collective-permute-start.29 = (bf16[128,1024]{0,1:T(8,128)(2,1)S(1)}, bf16[128,1024]{0,1:T(8,128)(2,1)S(1)}, u32[]{:S(2)}, u32[]{:S(2)}) collective-permute-start(bf16[128,1024]{0,1:T(8,128)(2,1)S(1)} %add_convert_fusion.11), channel_id=1, source_target_pairs={{0,8},{8,16},{16,24},{24,28},{28,20},{20,12},{12,4},{4,0},{1,9},{9... | collective-permute-start | bytes 786440 | tf_op jit(solution)/shard_map/ppermute | solution.py:124
  581.0 19.4 %collective-permute-start.32 = (bf16[128,1024]{0,1:T(8,128)(2,1)S(1)}, bf16[128,1024]{0,1:T(8,128)(2,1)S(1)}, u32[]{:S(2)}, u32[]{:S(2)}) collective-permute-start(bf16[128,1024]{0,1:T(8,128)(2,1)S(1)} %get-tuple-element.88), channel_id=1, source_target_pairs={{8,0},{16,8},{24,16},{28,24},{20,28},{12,20},{4,12},{0,4},{9,1},{1... | collective-permute-start | bytes 786440 | tf_op jit(solution)/shard_map/ppermute | solution.py:124
  585.2 19.2 %collective-permute-start.30 = (bf16[128,1024]{0,1:T(8,128)(2,1)S(1)}, bf16[128,1024]{0,1:T(8,128)(2,1)S(1)}, u32[]{:S(2)}, u32[]{:S(2)}) collective-permute-start(bf16[128,1024]{0,1:T(8,128)(2,1)S(1)} %get-tuple-element.87), channel_id=1, source_target_pairs={{0,8},{8,16},{16,24},{24,28},{28,20},{20,12},{12,4},{4,0},{1,9},{9... | collective-permute-start | bytes 786440 | tf_op jit(solution)/shard_map/ppermute | solution.py:124
  600.5 20.2 %collective-permute-start.33 = (bf16[128,1024]{0,1:T(8,128)(2,1)S(1)}, bf16[128,1024]{0,1:T(8,128)(2,1)S(1)}, u32[]{:S(2)}, u32[]{:S(2)}) collective-permute-start(bf16[128,1024]{0,1:T(8,128)(2,1)S(1)} %add_convert_fusion.8), channel_id=1, source_target_pairs={{8,0},{16,8},{24,16},{28,24},{20,28},{12,20},{4,12},{0,4},{9,1},{1... | collective-permute-start | bytes 786440 | tf_op jit(solution)/shard_map/ppermute | solution.py:124
  602.4 18.5 %copy-start.30 = (f32[1024,2,256]{2,0,1:T(8,128)}, f32[1024,2,256]{2,0,1:T(8,128)S(1)}, u32[]{:S(2)}) copy-start(f32[1024,2,256]{2,0,1:T(8,128)S(1)} %maximum_add_fusion.5) | copy-start | bytes 6291460
  602.5 20.1 %collective-permute-start.26 = (bf16[1024,1,256]{2,0,1:T(8,128)(2,1)S(1)}, bf16[1024,1,256]{2,0,1:T(8,128)(2,1)S(1)}, u32[]{:S(2)}, u32[]{:S(2)}) collective-permute-start(bf16[1024,1,256]{2,0,1:T(8,128)(2,1)S(1)} %dynamic-slice_convert_fusion), channel_id=1, source_target_pairs={{0,2},{1,3},{2,0},{3,1},{4,6},{5,7},{6,4},{7,5},{8,10},{9,11},{10,... | collective-permute-start | bytes 1572872 | tf_op jit(solution)/shard_map/ppermute | solution.py:133
  (92 other events, 351.1 us)
Sparse Core Ops, SparseCore 0:
  13.4 80.6 all-gather.1
  450.4 119.6 all-reduce.2
  573.7 100.0 reduce-scatter.3
where the time goes:
time: 692 us; the launch traced here: 684 us
  waiting for transfers between devices  223 us (32%)
  matrix products  145 us (21%)
  other arithmetic  122 us (18%)
  local copies, waits for them, and re-layouts  90.8 us (13%)
  blocking collectives  43.3 us (6%)
  starting transfers between devices  30.4 us (4%)
  between operations  29.9 us (4%)
    ppermute x20, waiting for transfers between devices, swap(): return lax.ppermute(value, 'tensor', [(i, i ^ bit) for i in range(n)])  82.7 us
    psum x1, waiting for transfers between devices, shards(): sums = lax.psum(sums, ('dp', 'tensor'))  49.7 us
    unnamed x4, waiting for transfers between devices  47.9 us
    unnamed x253, local copies, waits for them, and re-layouts  38.4 us
    ppermute x7, waiting for transfers between devices, scatter(): run = lax.ppermute(run.astype(bf16), 'dp', way).astype(f32)  35.6 us
    all_gather x1, blocking collectives, shards(): small = lax.all_gather(small, 'dp', axis=1, tiled=True)  31.2 us
    dot_general x8, matrix products, mm(): return jnp.dot(left, right, preferred_element_type=f32)  26.2 us
    dot_general x4, matrix products, mm_lt(): return jnp.einsum('ki,kj->ij', left, right, preferred_element_type=f32)  25 us
  transfers between devices with their start and end apart: 37, of which 18 were waited for; matrix products, arithmetic and copies ran while one was open for 36% of the time, Pallas kernels for 0%

commit v1 on v0

--- a/solution.py
+++ b/solution.py
@@ -10,6 +10,27 @@
 masked = -1000000000.0
 f32 = jnp.float32
 bf16 = jnp.bfloat16
+
+
+def gather_around(x, axis, dim):
+    devices, index, span = (lax.axis_size(axis), lax.axis_index(axis), x.shape[dim])
+    upward = [(i, (i + 1) % devices) for i in range(devices)]
+    left = [(i, (i - 1) % devices) for i in range(devices)]
+    whole = jnp.zeros((*x.shape[:dim], devices * span, *x.shape[dim + 1 :]), x.dtype)
+    whole = lax.dynamic_update_slice_in_dim(whole, x, index * span, axis=dim)
+    from_left = from_right = x
+    halfway = devices // 2
+    for lap in range(1, halfway + 1):
+        from_left = lax.ppermute(from_left, axis, upward)
+        whole = lax.dynamic_update_slice_in_dim(
+            whole, from_left, (index - lap) % devices * span, axis=dim
+        )
+        if lap < devices - halfway:
+            from_right = lax.ppermute(from_right, axis, left)
+            whole = lax.dynamic_update_slice_in_dim(
+                whole, from_right, (index + lap) % devices * span, axis=dim
+            )
+    return whole
 
 
 def sinusoid(values, width):
@@ -188,7 +209,7 @@
     small = jnp.concatenate(
         [cond_part, gain_attn.astype(f32)[None], gain_mlp.astype(f32)[None]], axis=0
     )
-    small = lax.all_gather(small, "dp", axis=1, tiled=True)
+    small = gather_around(small, "dp", 1)
     n_seqs = n_dp * seqs_dev
     cond = lax.dynamic_slice_in_dim(small, me_dp * seqs_dev, seqs_dev, 0)
     attn_g, mlp_g = (small[n_seqs], small[n_seqs + 1])

time: 692 us -> 711 us (1.027)
  blocking collectives: 43.3 us -> 13.1 us
  waiting for transfers between devices: 223 us -> 242 us
  starting transfers between devices: 30.4 us -> 49.1 us
    all_gather x1 -> x0, blocking collectives: 31.2 us -> none  [shards(): small = lax.all_gather(small, 'dp', axis=1, tiled=True)]
    ppermute x0 -> x7, starting transfers between devices: none -> 14.3 us  [the longest x3 12.7 us: gather_around(): from_right = lax.ppermute(from_right, axis, left)]
    ppermute x0 -> x7, waiting for transfers between devices: none -> 10.5 us  [the longest x4 10.5 us: gather_around(): from_left = lax.ppermute(from_left, axis, upward)]
    dot_general x12, matrix products: 21.7 us -> 30.2 us  [mm_rt(): return jnp.einsum('ik,jk->ij', left, right, preferred_element_type=f32)]
    ppermute x4, waiting for transfers between devices: 7.25 us -> 15.7 us  [gather(): from_left = lax.ppermute(from_left, 'dp', self.right)]
    unnamed x253 -> x235, local copies, waits for them, and re-layouts: 38.4 us -> 40.7 us
  transfers between devices with their start and end apart: 37 -> 44, of which waited for: 18 -> 22; matrix products, arithmetic and copies ran while one was open for 36% -> 37% of each run, Pallas kernels for 0% -> 0%
where the time goes in v1:
time: 711 us; the launch traced here: 703 us
  waiting for transfers between devices  242 us (34%)
  matrix products  147 us (21%)
  other arithmetic  126 us (18%)
  local copies, waits for them, and re-layouts  96 us (14%)
  starting transfers between devices  49.1 us (7%)
  between operations  29.9 us (4%)
  blocking collectives  13.1 us (2%)
    ppermute x20, waiting for transfers between devices, swap(): return lax.ppermute(value, 'tensor', [(i, i ^ bit) for i in range(n)])  80.8 us
    psum x1, waiting for transfers between devices, shards(): sums = lax.psum(sums, ('dp', 'tensor'))  51.3 us
    unnamed x4, waiting for transfers between devices  47.9 us
    unnamed x235, local copies, waits for them, and re-layouts  40.7 us
    ppermute x7, waiting for transfers between devices, scatter(): run = lax.ppermute(run.astype(bf16), 'dp', way).astype(f32)  35.4 us
    dot_general x12, matrix products, mm_rt(): return jnp.einsum('ik,jk->ij', left, right, preferred_element_type=f32)  30.2 us
    dot_general x8, matrix products, mm(): return jnp.dot(left, right, preferred_element_type=f32)  29.7 us
    dot_general x4, matrix products, mm_lt(): return jnp.einsum('ki,kj->ij', left, right, preferred_element_type=f32)  24.7 us
  transfers between devices with their start and end apart: 44, of which 22 were waited for; matrix products, arithmetic and copies ran while one was open for 37% of the time, Pallas kernels for 0%

profile of v1, /device:TPU:0, one launch (start us, length us, event | category | flops | bytes accessed | tf_op | source)
XLA Modules:
  0.0 703.4 jit_solution(6478496872982605712)
XLA Ops:
  10.1 13.1 %all-reduce = s32[16]{0:T(128)S(1)} all-reduce(s32[16]{0:T(128)S(1)} %dynamic-update-slice), channel_id=1, replica_groups=mesh['dp'=8,'tensor'=4] {'dp'}, use_global_device_ids=true, to_apply=%add | all-reduce | flops 16 | bytes 128
  25.7 3.2 collective-permute-start.1
  38.5 4.8 slice_bitcast_fusion.3
  43.3 17.2 %multiply_sine_fusion.1 = (f32[1024,512]{1,0:T(8,128)}, f32[1024,512]{1,0:T(8,128)}, f32[1024,512]{1,0:T(8,128)}, f32[1024,512]{1,0:T(8,128)}) fusion(f32[512]{0:T(512)S(1)} %multiply_exponential_fusion, f32[1024]{0:T(1024)S(1)} %fusion.204, f32[1024]{0:T(1024)S(1)} %fusion.201), kind=kLoop, calls=%fused_computation.119 | loop fusion | flops 1048576 | bytes 8398848 | tf_op jit(solution)/shard_map/sin | solution.py:40
  72.4 4.7 collective-permute-start.3
  79.1 4.8 collective-permute-start.5
  85.6 6.7 collective-permute-done.6
  92.4 3.5 fusion.222
  99.2 11.0 %collective-permute-done.10 = bf16[128,1024]{0,1:T(8,128)(2,1)S(1)} collective-permute-done((bf16[128,1024]{0,1:T(8,128)(2,1)S(1)}, bf16[128,1024]{0,1:T(8,128)(2,1)S(1)}, u32[]{:S(2)}, u32[]{:S(2)}) %collective-permute-start.10) | collective-permute-done | bytes 262176 | tf_op jit(solution)/shard_map/ppermute | solution.py:125
  110.1 3.0 collective-permute-start.12
  116.0 3.1 collective-permute-done.12
  119.1 2.9 collective-permute-start.13
  126.6 3.2 convolution_convert_fusion.1
  130.0 7.5 %fusion.238 = (f32[4,1024]{1,0:T(4,128)S(1)}, f32[4,1024,1024]{1,2,0:T(8,128)}) fusion(bf16[1024,4,64]{0,2,1:T(8,128)(2,1)S(1)} %bitcast.178, bf16[1024,4,64]{0,2,1:T(8,128)(2,1)S(1)} %bitcast.176, pred[1024,1024]{0,1:T(8,128)(4,1)S(1)} %broadcast_compare_fusion.1), kind=kOutput, calls=%fused_computation.447 | convolution fusion | flops 549449728 | bytes 18890752 | tf_op jit(solution)/shard_map/qhe,khe->hqk/dot_general | solution.py:69
  137.5 8.0 %fusion = f32[4,1024]{1,0:T(4,128)S(1)} fusion(f32[4,1024,1024]{1,2,0:T(8,128)} %get-tuple-element.154, f32[4,1024]{1,0:T(4,128)S(1)} %get-tuple-element.153), kind=kLoop, calls=%fused_computation.12 | loop fusion | flops 8384512 | bytes 16809984 | tf_op jit(solution)/shard_map/reduce_sum | solution.py:73
  145.5 7.9 %fusion.144 = bf16[4,64,1024]{2,1,0:T(8,128)(2,1)S(1)} fusion(bf16[1024,4,64]{0,2,1:T(8,128)(2,1)S(1)} %bitcast.188, f32[4,1024,1024]{1,2,0:T(8,128)} %get-tuple-element.154, f32[4,1024]{1,0:T(4,128)S(1)} %fusion, f32[4,1024]{1,0:T(4,128)S(1)} %get-tuple-element.153), kind=kOutput, calls=%fused_computation.250 | convolution fusion | flops 549715968 | bytes 17858560 | tf_op jit(solution)/shard_map/hqk,khe->qhe/dot_general | solution.py:75
  159.8 23.7 %collective-permute-done.15 = bf16[512,1024]{1,0:T(8,128)(2,1)S(1)} collective-permute-done((bf16[512,1024]{1,0:T(8,128)(2,1)S(1)}, bf16[512,1024]{1,0:T(8,128)(2,1)S(1)}, u32[]{:S(2)}, u32[]{:S(2)}) %collective-permute-start.15) | collective-permute-done | bytes 1048608 | tf_op jit(solution)/shard_map/ppermute | solution.py:154
  188.3 4.2 fusion.68
  192.5 5.0 multiply_convert_fusion.4
  197.6 3.9 fusion.17
  202.8 2.6 collective-permute-done.24
  216.9 2.9 copy.144
  219.7 13.5 %collective-permute-done.25 = bf16[512,1024]{1,0:T(8,128)(2,1)} collective-permute-done((bf16[512,1024]{1,0:T(8,128)(2,1)}, bf16[512,1024]{1,0:T(8,128)(2,1)}, u32[]{:S(2)}, u32[]{:S(2)}) %collective-permute-start.25) | collective-permute-done | bytes 1048608 | tf_op jit(solution)/shard_map/ppermute | solution.py:154
  233.3 3.2 multiply_reduce_fusion.11
  236.6 3.8 fusion.219
  240.4 3.7 fusion.225
  246.4 2.7 fusion.133
  249.1 2.9 fusion.124
  252.0 7.8 %multiply_reduce_fusion.1 = (f32[4,1024]{1,0:T(4,128)S(1)}, f32[4,1024,1024]{1,2,0:T(8,128)}) fusion(f32[4,1024,1024]{1,2,0:T(8,128)S(1)} %bitcast.171, f32[4,1024]{1,0:T(4,128)S(1)} %log_add_fusion.1, bf16[1024,4,64]{0,2,1:T(8,128)(2,1)S(1)} %bitcast.183, bf16[1024,4,64]{0,2,1:T(8,128)(2,1)S(1)} %bitcast.189), kind=kOutput, calls=%fused_computation.4 | convolution fusion | flops 549449728 | bytes 34635776 | tf_op jit(solution)/shard_map/qhe,khe->hqk/dot_general | solution.py:83
  259.9 7.9 %multiply_convert_fusion.1 = bf16[4,1024,1024]{1,2,0:T(8,128)(2,1)S(1)} fusion(f32[4,1024,1024]{1,2,0:T(8,128)} %get-tuple-element.158, f32[4,1024,1024]{1,2,0:T(8,128)S(1)} %bitcast.171, f32[4,1024]{1,0:T(4,128)S(1)} %get-tuple-element.157, f32[4,1024]{1,0:T(4,128)S(1)} %log_add_fusion.1), kind=kLoop, calls=%fused_computation.3 | loop fusion | flops 16777216 | bytes 41975808 | tf_op jit(solution)/shard_map/convert_element_type | solution.py:86
  267.7 2.7 fusion.137
  272.8 5.2 multiply_reduce_fusion.3
  278.0 3.5 subtract_multiply_fusion.1
  282.8 3.3 convolution_convert_fusion
  287.8 7.8 %fusion.239 = (f32[4,1024]{1,0:T(4,128)S(1)}, f32[4,1024,1024]{1,2,0:T(8,128)}) fusion(bf16[1024,4,64]{0,2,1:T(8,128)(2,1)S(1)} %bitcast.174, bf16[1024,4,64]{0,2,1:T(8,128)(2,1)S(1)} %bitcast.172, pred[1024,1024]{0,1:T(8,128)(4,1)S(1)} %copy-done.9), kind=kOutput, calls=%fused_computation.448 | convolution fusion | flops 549449728 | bytes 18890752 | tf_op jit(solution)/shard_map/qhe,khe->hqk/dot_general | solution.py:69
  295.6 8.0 %fusion.1 = f32[4,1024]{1,0:T(4,128)S(1)} fusion(f32[4,1024,1024]{1,2,0:T(8,128)} %get-tuple-element.161, f32[4,1024]{1,0:T(4,128)S(1)} %get-tuple-element.160), kind=kLoop, calls=%fused_computation.13 | loop fusion | flops 8384512 | bytes 16809984 | tf_op jit(solution)/shard_map/reduce_sum | solution.py:73
  303.6 7.4 %fusion.143 = bf16[4,64,1024]{2,1,0:T(8,128)(2,1)S(1)} fusion(bf16[1024,4,64]{0,2,1:T(8,128)(2,1)S(1)} %bitcast.186, f32[4,1024,1024]{1,2,0:T(8,128)} %get-tuple-element.161, f32[4,1024]{1,0:T(4,128)S(1)} %fusion.1, f32[4,1024]{1,0:T(4,128)S(1)} %get-tuple-element.160), kind=kOutput, calls=%fused_computation.249 | convolution fusion | flops 549715968 | bytes 17858560 | tf_op jit(solution)/shard_map/hqk,khe->qhe/dot_general | solution.py:75
  317.4 23.7 %collective-permute-done.20 = bf16[512,1024]{1,0:T(8,128)(2,1)S(1)} collective-permute-done((bf16[512,1024]{1,0:T(8,128)(2,1)S(1)}, bf16[512,1024]{1,0:T(8,128)(2,1)S(1)}, u32[]{:S(2)}, u32[]{:S(2)}) %collective-permute-start.20) | collective-permute-done | bytes 1048608 | tf_op jit(solution)/shard_map/ppermute | solution.py:154
  343.3 4.7 fusion.67
  347.9 2.7 slice.402
  352.9 2.8 concatenate.137
  359.2 5.5 multiply_convert_fusion.2
  364.7 3.7 fusion.23
  385.4 3.9 add_convert_fusion
  396.9 3.1 copy.145
  400.0 9.4 %fusion.89 = bf16[1024,1024]{0,1:T(8,128)(2,1)} fusion(bf16[1024,1024]{1,0:T(8,128)(2,1)} %get-tuple-element.162, bf16[1024,1024]{1,0:T(8,128)(2,1)} %copy-done.100, bf16[1024,1024]{1,0:T(8,128)(2,1)} %fusion.67, bf16[1024,1024]{1,0:T(8,128)(2,1)} %fusion.68), kind=kOutput, calls=%fused_computation.203 | convolution fusion | flops 4312793088 | bytes 10485760 | tf_op jit(solution)/shard_map/ki,kj->ij/dot_general | solution.py:101
  409.4 5.6 collective-permute-done.30
  417.6 4.0 fusion.220
  421.7 9.2 %fusion.94 = bf16[1024,1024]{0,1:T(8,128)(2,1)} fusion(bf16[1024,1024]{1,0:T(8,128)(2,1)} %copy-done.99, bf16[1024,1024]{1,0:T(8,128)(2,1)} %copy-done.98, bf16[512,1024]{1,0:T(8,128)(2,1)} %collective-permute-done.21, bf16[512,1024]{1,0:T(8,128)(2,1)} %multiply_convert_fusion.6, bf16[512,1024]{1,0:T(8,128)(2,1)} %collective-permute-done.16, ...), kind=kOutput, calls=%fused_computation.204 | convolution fusion | flops 4321181696 | bytes 10485760 | tf_op jit(solution)/shard_map/ki,kj->ij/dot_general | solution.py:101
  433.4 3.3 fusion.127
  436.7 7.6 %multiply_reduce_fusion = (f32[4,1024]{1,0:T(4,128)S(1)}, f32[4,1024,1024]{1,2,0:T(8,128)}) fusion(f32[4,1024,1024]{1,2,0:T(8,128)S(1)} %bitcast.169, f32[4,1024]{1,0:T(4,128)S(1)} %log_add_fusion, bf16[1024,4,64]{0,2,1:T(8,128)(2,1)S(1)} %bitcast.185, bf16[1024,4,64]{0,2,1:T(8,128)(2,1)S(1)} %bitcast.187), kind=kOutput, calls=%fused_computation.1 | convolution fusion | flops 549449728 | bytes 34635776 | tf_op jit(solution)/shard_map/qhe,khe->hqk/dot_general | solution.py:83
  444.3 7.9 %multiply_convert_fusion = bf16[4,1024,1024]{1,2,0:T(8,128)(2,1)S(1)} fusion(f32[4,1024,1024]{1,2,0:T(8,128)} %get-tuple-element.165, f32[4,1024,1024]{1,2,0:T(8,128)S(1)} %bitcast.169, f32[4,1024]{1,0:T(4,128)S(1)} %get-tuple-element.164, f32[4,1024]{1,0:T(4,128)S(1)} %log_add_fusion), kind=kLoop, calls=%fused_computation | loop fusion | flops 16777216 | bytes 41975808 | tf_op jit(solution)/shard_map/convert_element_type | solution.py:86
  452.2 2.7 fusion.139
  457.3 4.3 multiply_reduce_fusion.2
  466.4 4.1 pad_maximum_fusion
  470.5 6.7 copy.139
  499.1 7.6 %collective-permute-done.28 = bf16[1024,1,256]{2,0,1:T(8,128)(2,1)} collective-permute-done((bf16[1024,1,256]{2,0,1:T(8,128)(2,1)}, bf16[1024,1,256]{2,0,1:T(8,128)(2,1)}, u32[]{:S(2)}, u32[]{:S(2)}) %collective-permute-start.28) | collective-permute-done | bytes 524320 | tf_op jit(solution)/shard_map/ppermute | solution.py:154
  509.3 2.7 slice.403
  518.8 3.4 fusion.99
  538.4 51.3 %all-reduce.3.cloned.1.call-done = f32[18,1024]{1,0:T(8,128)} async-done(((f32[18,1024]{1,0:T(8,128)}), f32[18,1024]{1,0:T(8,128)}) %all-reduce.3.cloned.1.call-update) | async-done | bytes 73744 | tf_op jit(solution)/shard_map/psum | solution.py:333
  592.6 3.3 collective-permute-start.36
  605.3 14.7 %collective-permute-done.39 = bf16[128,1024]{0,1:T(8,128)(2,1)S(1)} collective-permute-done((bf16[128,1024]{0,1:T(8,128)(2,1)S(1)}, bf16[128,1024]{0,1:T(8,128)(2,1)S(1)}, u32[]{:S(2)}, u32[]{:S(2)}) %collective-permute-start.39) | collective-permute-done | bytes 262176 | tf_op jit(solution)/shard_map/ppermute | solution.py:145
  624.0 16.4 %collective-permute-done.40 = bf16[128,1024]{0,1:T(8,128)(2,1)S(1)} collective-permute-done((bf16[128,1024]{0,1:T(8,128)(2,1)S(1)}, bf16[128,1024]{0,1:T(8,128)(2,1)S(1)}, u32[]{:S(2)}, u32[]{:S(2)}) %collective-permute-start.40) | collective-permute-done | bytes 262176 | tf_op jit(solution)/shard_map/ppermute | solution.py:145
  645.5 47.9 %reduce-scatter.4.cloned.1.call-done = bf16[128,2048]{1,0:T(8,128)(2,1)} async-done(((bf16[1024,2048]{1,0:T(8,128)(2,1)}), bf16[128,2048]{1,0:T(8,128)(2,1)}) %reduce-scatter.4.cloned.1.call-update) | async-done | bytes 524304
  (458 shorter events, 181.4 us)
Async XLA Ops:
  7.2 16.8 %copy-start = (bf16[256,128]{1,0:T(8,128)(2,1)S(1)}, bf16[256,128]{1,0:T(8,128)(2,1)}, u32[]{:S(2)}) copy-start(bf16[256,128]{1,0:T(8,128)(2,1)} %param.30) | copy-start | bytes 196612
  7.2 24.6 %copy-start.84 = (bf16[256,128]{1,0:T(8,128)(2,1)S(1)}, bf16[256,128]{1,0:T(8,128)(2,1)}, u32[]{:S(2)}) copy-start(bf16[256,128]{1,0:T(8,128)(2,1)} %param.27) | copy-start | bytes 196612
  7.2 27.4 %copy-start.78 = (bf16[128,1024]{1,0:T(8,128)(2,1)S(1)}, bf16[128,1024]{1,0:T(8,128)(2,1)}, u32[]{:S(2)}) copy-start(bf16[128,1024]{1,0:T(8,128)(2,1)} %param.28) | copy-start | bytes 786436
  7.2 185.3 %all-gather.2.cloned.1.call-start = ((), (), s32[]{:S(2)}) async-start(), calls=%async_computation.1 | async-start | bytes 4718592 | tf_op jit(solution)/shard_map/all_gather | solution.py:205
  24.2 48.1 %collective-permute-start = (f32[18,128]{1,0:T(8,128)S(1)}, f32[18,128]{1,0:T(8,128)S(1)}, u32[]{:S(2)}, u32[]{:S(2)}) collective-permute-start(f32[18,128]{1,0:T(8,128)S(1)} %get-tuple-element.128), channel_id=1, source_target_pairs={{0,4},{4,8},{8,12},{12,16},{16,20},{20,24},{24,28},{28,0},{1,5},{5... | collective-permute-start | bytes 27656 | tf_op jit(solution)/shard_map/ppermute | solution.py:24
  25.7 46.6 %collective-permute-start.1 = (f32[18,128]{1,0:T(8,128)S(1)}, f32[18,128]{1,0:T(8,128)S(1)}, u32[]{:S(2)}, u32[]{:S(2)}) collective-permute-start(f32[18,128]{1,0:T(8,128)S(1)} %get-tuple-element.128), channel_id=1, source_target_pairs={{0,28},{4,0},{8,4},{12,8},{16,12},{20,16},{24,20},{28,24},{1,29},{... | collective-permute-start | bytes 27656 | tf_op jit(solution)/shard_map/ppermute | solution.py:29
  32.6 63.9 %collective-permute-start.7 = (bf16[128,1024]{0,1:T(8,128)(2,1)S(1)}, bf16[128,1024]{0,1:T(8,128)(2,1)S(1)}, u32[]{:S(2)}, u32[]{:S(2)}) collective-permute-start(bf16[128,1024]{0,1:T(8,128)(2,1)S(1)} %get-tuple-element.117), channel_id=1, source_target_pairs={{8,0},{16,8},{24,16},{28,24},{20,28},{12,20},{4,12},{0,4},{9,1},{1... | collective-permute-start | bytes 786440 | tf_op jit(solution)/shard_map/ppermute | solution.py:127
  32.6 64.0 %collective-permute-start.8 = (bf16[128,1024]{0,1:T(8,128)(2,1)S(1)}, bf16[128,1024]{0,1:T(8,128)(2,1)S(1)}, u32[]{:S(2)}, u32[]{:S(2)}) collective-permute-start(bf16[128,1024]{0,1:T(8,128)(2,1)S(1)} %get-tuple-element.117), channel_id=1, source_target_pairs={{0,8},{8,16},{16,24},{24,28},{28,20},{20,12},{12,4},{4,0},{1,9},{9... | collective-permute-start | bytes 786440 | tf_op jit(solution)/shard_map/ppermute | solution.py:125
  35.6 554.0 %all-reduce.3.cloned.1.call-start = ((), (), s32[]{:S(2)}) async-start(), calls=%async_computation.2 | async-start | bytes 196608 | tf_op jit(solution)/shard_map/psum | solution.py:333
  43.3 23.8 %copy-start.85 = (s32[8]{0:T(128)S(1)}, s32[8]{0:T(128)}, u32[]{:S(2)}) copy-start(s32[8]{0:T(128)} %constant.359.clone) | copy-start | bytes 100
  72.3 6.8 collective-permute-start.2
  72.4 6.7 collective-permute-start.3
  79.1 6.5 collective-permute-start.4
  79.1 6.5 collective-permute-start.5
  85.6 6.7 collective-permute-start.6
  95.9 87.7 %copy-start.5 = (f32[1024,1024]{1,0:T(8,128)}, f32[1024,1024]{1,0:T(8,128)S(1)}, u32[]{:S(2)}) copy-start(f32[1024,1024]{1,0:T(8,128)S(1)} %get-tuple-element.76) | copy-start | bytes 12582916
  96.5 18.0 %collective-permute-start.9 = (bf16[128,1024]{0,1:T(8,128)(2,1)S(1)}, bf16[128,1024]{0,1:T(8,128)(2,1)S(1)}, u32[]{:S(2)}, u32[]{:S(2)}) collective-permute-start(bf16[128,1024]{0,1:T(8,128)(2,1)S(1)} %collective-permute-done.7), channel_id=1, source_target_pairs={{8,0},{16,8},{24,16},{28,24},{20,28},{12,20},{4,12},{0,4},{9,1},{1... | collective-permute-start | bytes 786440 | tf_op jit(solution)/shard_map/ppermute | solution.py:127
  96.6 13.6 %collective-permute-start.10 = (bf16[128,1024]{0,1:T(8,128)(2,1)S(1)}, bf16[128,1024]{0,1:T(8,128)(2,1)S(1)}, u32[]{:S(2)}, u32[]{:S(2)}) collective-permute-start(bf16[128,1024]{0,1:T(8,128)(2,1)S(1)} %collective-permute-done.8), channel_id=1, source_target_pairs={{0,8},{8,16},{16,24},{24,28},{28,20},{20,12},{12,4},{4,0},{1,9},{9... | collective-permute-start | bytes 786440 | tf_op jit(solution)/shard_map/ppermute | solution.py:125
  99.1 30.7 %copy-start.52 = (bf16[1024,1024]{1,0:T(8,128)(2,1)}, bf16[1024,1024]{1,0:T(8,128)(2,1)S(1)}, u32[]{:S(2)}) copy-start(bf16[1024,1024]{1,0:T(8,128)(2,1)S(1)} %multiply_convert_fusion.5) | copy-start | bytes 6291460
  110.1 9.0 %collective-permute-start.12 = (bf16[128,1024]{0,1:T(8,128)(2,1)S(1)}, bf16[128,1024]{0,1:T(8,128)(2,1)S(1)}, u32[]{:S(2)}, u32[]{:S(2)}) collective-permute-start(bf16[128,1024]{0,1:T(8,128)(2,1)S(1)} %collective-permute-done.10), channel_id=1, source_target_pairs={{0,8},{8,16},{16,24},{24,28},{28,20},{20,12},{12,4},{4,0},{1,9},{9... | collective-permute-start | bytes 786440 | tf_op jit(solution)/shard_map/ppermute | solution.py:125
  114.5 8.3 %collective-permute-start.11 = (bf16[128,1024]{0,1:T(8,128)(2,1)S(1)}, bf16[128,1024]{0,1:T(8,128)(2,1)S(1)}, u32[]{:S(2)}, u32[]{:S(2)}) collective-permute-start(bf16[128,1024]{0,1:T(8,128)(2,1)S(1)} %collective-permute-done.9), channel_id=1, source_target_pairs={{8,0},{16,8},{24,16},{28,24},{20,28},{12,20},{4,12},{0,4},{9,1},{1... | collective-permute-start | bytes 786440 | tf_op jit(solution)/shard_map/ppermute | solution.py:127
  119.1 6.8 collective-permute-start.13
  130.0 15.5 %copy-start.50 = (bf16[1024,256]{0,1:T(8,128)(2,1)}, bf16[1024,256]{0,1:T(8,128)(2,1)S(1)}, u32[]{:S(2)}) copy-start(bf16[1024,256]{0,1:T(8,128)(2,1)S(1)} %get-tuple-element.95) | copy-start | bytes 1572868
  155.1 2.7 collective-permute-start.14
  158.3 25.3 %collective-permute-start.15 = (bf16[512,1024]{1,0:T(8,128)(2,1)S(1)}, bf16[512,1024]{1,0:T(8,128)(2,1)S(1)}, u32[]{:S(2)}, u32[]{:S(2)}) collective-permute-start(bf16[512,1024]{1,0:T(8,128)(2,1)S(1)} %add_convert_fusion.5), channel_id=1, source_target_pairs={{0,2},{1,3},{2,0},{3,1},{4,6},{5,7},{6,4},{7,5},{8,10},{9,11},{10,... | collective-permute-start | bytes 3145736 | tf_op jit(solution)/shard_map/ppermute | solution.py:154
  184.7 7.8 %collective-permute-start.16 = (bf16[512,1024]{1,0:T(8,128)(2,1)S(1)}, bf16[512,1024]{1,0:T(8,128)(2,1)}, u32[]{:S(2)}, u32[]{:S(2)}) collective-permute-start(bf16[512,1024]{1,0:T(8,128)(2,1)S(1)} %multiply_convert_fusion.7), channel_id=1, source_target_pairs={{0,1},{1,0},{2,3},{3,2},{4,5},{5,4},{6,7},{7,6},{8,9},{9,8},{10,11... | collective-permute-start | bytes 3145736 | tf_op jit(solution)/shard_map/ppermute | solution.py:154
  197.6 13.4 %copy-start.100 = (bf16[1024,1024]{1,0:T(8,128)(2,1)}, bf16[1024,1024]{1,0:T(8,128)(2,1)S(1)}, u32[]{:S(2)}) copy-start(bf16[1024,1024]{1,0:T(8,128)(2,1)S(1)} %get-tuple-element.155) | copy-start | bytes 6291460
  202.8 2.7 collective-permute-start.24
  207.8 25.5 %collective-permute-start.25 = (bf16[512,1024]{1,0:T(8,128)(2,1)}, bf16[512,1024]{1,0:T(8,128)(2,1)}, u32[]{:S(2)}, u32[]{:S(2)}) collective-permute-start(bf16[512,1024]{1,0:T(8,128)(2,1)} %add_convert_fusion.1), channel_id=1, source_target_pairs={{0,2},{1,3},{2,0},{3,1},{4,6},{5,7},{6,4},{7,5},{8,10},{9,11},{10,... | collective-permute-start | bytes 3145736 | tf_op jit(solution)/shard_map/ppermute | solution.py:154
  219.7 16.8 %copy-start.15 = (f32[512,1024]{1,0:T(8,128)S(1)}, f32[512,1024]{1,0:T(8,128)}, u32[]{:S(2)}) copy-start(f32[512,1024]{1,0:T(8,128)} %copy.144) | copy-start | bytes 6291460
  236.5 12.5 %slice-start.4 = ((s8[16777216]{0:T(1024)(128)(4,1)}), s8[4194304]{0:T(1024)(128)(4,1)S(1)}, s32[]{:S(2)}) async-start(s8[16777216]{0:T(1024)(128)(4,1)} %bitcast.170), calls=%async_computation.8 | async-start | bytes 8388608
  236.6 12.5 %slice-start.5 = ((s8[16777216]{0:T(1024)(128)(4,1)}), s8[4194304]{0:T(1024)(128)(4,1)S(1)}, s32[]{:S(2)}) async-start(s8[16777216]{0:T(1024)(128)(4,1)} %bitcast.170), calls=%async_computation.9 | async-start | bytes 8388608
  240.4 5.9 collective-permute-start.26
  252.0 20.0 %copy-start.62 = (bf16[4,64,1024]{2,1,0:T(8,128)(2,1)}, bf16[4,64,1024]{2,1,0:T(8,128)(2,1)S(1)}, u32[]{:S(2)}) copy-start(bf16[4,64,1024]{2,1,0:T(8,128)(2,1)S(1)} %fusion.124) | copy-start | bytes 1572868
  286.3 17.3 %copy-start.48 = (bf16[1024,256]{0,1:T(8,128)(2,1)}, bf16[1024,256]{0,1:T(8,128)(2,1)S(1)}, u32[]{:S(2)}) copy-start(bf16[1024,256]{0,1:T(8,128)(2,1)S(1)} %get-tuple-element.98) | copy-start | bytes 1572868
  312.7 2.7 collective-permute-start.19
  315.9 25.3 %collective-permute-start.20 = (bf16[512,1024]{1,0:T(8,128)(2,1)S(1)}, bf16[512,1024]{1,0:T(8,128)(2,1)S(1)}, u32[]{:S(2)}, u32[]{:S(2)}) collective-permute-start(bf16[512,1024]{1,0:T(8,128)(2,1)S(1)} %add_convert_fusion.3), channel_id=1, source_target_pairs={{0,2},{1,3},{2,0},{3,1},{4,6},{5,7},{6,4},{7,5},{8,10},{9,11},{10,... | collective-permute-start | bytes 3145736 | tf_op jit(solution)/shard_map/ppermute | solution.py:154
  343.3 15.7 %collective-permute-start.21 = (bf16[512,1024]{1,0:T(8,128)(2,1)}, bf16[512,1024]{1,0:T(8,128)(2,1)}, u32[]{:S(2)}, u32[]{:S(2)}) collective-permute-start(bf16[512,1024]{1,0:T(8,128)(2,1)} %multiply_convert_fusion.6), channel_id=1, source_target_pairs={{0,1},{1,0},{2,3},{3,2},{4,5},{5,4},{6,7},{7,6},{8,9},{9,8},{10,11... | collective-permute-start | bytes 3145736 | tf_op jit(solution)/shard_map/ppermute | solution.py:154
  358.5 118.7 %collective-permute-start.17 = (bf16[1024,2,256]{2,0,1:T(8,128)(2,1)}, bf16[1024,2,256]{2,0,1:T(8,128)(2,1)}, u32[]{:S(2)}, u32[]{:S(2)}) collective-permute-start(bf16[1024,2,256]{2,0,1:T(8,128)(2,1)} %fusion.154), channel_id=1, source_target_pairs={{0,1},{1,0},{2,3},{3,2},{4,5},{5,4},{6,7},{7,6},{8,9},{9,8},{10,11... | collective-permute-start | bytes 3145736 | tf_op jit(solution)/shard_map/ppermute | solution.py:154
  370.7 14.3 %collective-permute-start.29 = (bf16[512,1024]{1,0:T(8,128)(2,1)}, bf16[512,1024]{1,0:T(8,128)(2,1)}, u32[]{:S(2)}, u32[]{:S(2)}) collective-permute-start(bf16[512,1024]{1,0:T(8,128)(2,1)} %convolution_convert_fusion.2), channel_id=1, source_target_pairs={{0,1},{1,0},{2,3},{3,2},{4,5},{5,4},{6,7},{7,6},{8,9},{9,8},{10,11... | collective-permute-start | bytes 3145736 | tf_op jit(solution)/shard_map/ppermute | solution.py:154
  384.5 97.2 %collective-permute-start.27 = (bf16[1024,2,256]{2,0,1:T(8,128)(2,1)}, bf16[1024,2,256]{2,0,1:T(8,128)(2,1)}, u32[]{:S(2)}, u32[]{:S(2)}) collective-permute-start(bf16[1024,2,256]{2,0,1:T(8,128)(2,1)} %dynamic-slice_bitcast_fusion.1), channel_id=1, source_target_pairs={{0,1},{1,0},{2,3},{3,2},{4,5},{5,4},{6,7},{7,6},{8,9},{9,8},{10,11... | collective-permute-start | bytes 3145736 | tf_op jit(solution)/shard_map/ppermute | solution.py:154
  389.3 25.7 %collective-permute-start.30 = (bf16[512,1024]{1,0:T(8,128)(2,1)}, bf16[512,1024]{1,0:T(8,128)(2,1)}, u32[]{:S(2)}, u32[]{:S(2)}) collective-permute-start(bf16[512,1024]{1,0:T(8,128)(2,1)} %add_convert_fusion), channel_id=1, source_target_pairs={{0,2},{1,3},{2,0},{3,1},{4,6},{5,7},{6,4},{7,5},{8,10},{9,11},{10,... | collective-permute-start | bytes 3145736 | tf_op jit(solution)/shard_map/ppermute | solution.py:154
  417.5 15.8 %slice-start = ((s8[16777216]{0:T(1024)(128)(4,1)}), s8[4194304]{0:T(1024)(128)(4,1)S(1)}, s32[]{:S(2)}) async-start(s8[16777216]{0:T(1024)(128)(4,1)} %bitcast.168), calls=%async_computation.4 | async-start | bytes 8388608
  421.6 11.8 %slice-start.3 = ((s8[16777216]{0:T(1024)(128)(4,1)}), s8[4194304]{0:T(1024)(128)(4,1)S(1)}, s32[]{:S(2)}) async-start(s8[16777216]{0:T(1024)(128)(4,1)} %bitcast.168), calls=%async_computation.7 | async-start | bytes 8388608
  421.6 9.3 %collective-permute-start.31 = (bf16[512,1024]{1,0:T(8,128)(2,1)}, bf16[512,1024]{1,0:T(8,128)(2,1)S(1)}, u32[]{:S(2)}, u32[]{:S(2)}) collective-permute-start(bf16[512,1024]{1,0:T(8,128)(2,1)} %get-tuple-element.71), channel_id=1, source_target_pairs={{0,1},{1,0},{2,3},{3,2},{4,5},{5,4},{6,7},{7,6},{8,9},{9,8},{10,11... | collective-permute-start | bytes 3145736 | tf_op jit(solution)/shard_map/ppermute | solution.py:154
  436.7 19.8 %copy-start.68 = (bf16[4,64,1024]{2,1,0:T(8,128)(2,1)}, bf16[4,64,1024]{2,1,0:T(8,128)(2,1)S(1)}, u32[]{:S(2)}) copy-start(bf16[4,64,1024]{2,1,0:T(8,128)(2,1)S(1)} %fusion.127) | copy-start | bytes 1572868
  466.1 227.2 %reduce-scatter.4.cloned.1.call-start = ((), (), s32[]{:S(2)}) async-start(), calls=%async_computation.3 | async-start | bytes 4718592
  480.2 15.2 %collective-permute-start.18 = (bf16[1024,1,256]{2,0,1:T(8,128)(2,1)}, bf16[1024,1,256]{2,0,1:T(8,128)(2,1)}, u32[]{:S(2)}, u32[]{:S(2)}) collective-permute-start(bf16[1024,1,256]{2,0,1:T(8,128)(2,1)} %dynamic-slice_convert_fusion.3), channel_id=1, source_target_pairs={{0,2},{1,3},{2,0},{3,1},{4,6},{5,7},{6,4},{7,5},{8,10},{9,11},{10,... | collective-permute-start | bytes 1572872 | tf_op jit(solution)/shard_map/ppermute | solution.py:154
  489.0 23.1 %collective-permute-start.22 = (bf16[1024,2,256]{2,0,1:T(8,128)(2,1)}, bf16[1024,2,256]{2,0,1:T(8,128)(2,1)S(1)}, u32[]{:S(2)}, u32[]{:S(2)}) collective-permute-start(bf16[1024,2,256]{2,0,1:T(8,128)(2,1)} %fusion.150), channel_id=1, source_target_pairs={{0,1},{1,0},{2,3},{3,2},{4,5},{5,4},{6,7},{7,6},{8,9},{9,8},{10,11... | collective-permute-start | bytes 3145736 | tf_op jit(solution)/shard_map/ppermute | solution.py:154
  491.6 15.1 %collective-permute-start.28 = (bf16[1024,1,256]{2,0,1:T(8,128)(2,1)}, bf16[1024,1,256]{2,0,1:T(8,128)(2,1)}, u32[]{:S(2)}, u32[]{:S(2)}) collective-permute-start(bf16[1024,1,256]{2,0,1:T(8,128)(2,1)} %dynamic-slice_convert_fusion.1), channel_id=1, source_target_pairs={{0,2},{1,3},{2,0},{3,1},{4,6},{5,7},{6,4},{7,5},{8,10},{9,11},{10,... | collective-permute-start | bytes 1572872 | tf_op jit(solution)/shard_map/ppermute | solution.py:154
  493.7 13.0 %copy-start.23 = (f32[1024,2,256]{2,0,1:T(8,128)S(1)}, f32[1024,2,256]{2,0,1:T(8,128)}, u32[]{:S(2)}) copy-start(f32[1024,2,256]{2,0,1:T(8,128)} %maximum_add_fusion.4) | copy-start | bytes 6291460
  513.4 83.8 %collective-permute-start.23 = (bf16[1024,1,256]{2,0,1:T(8,128)(2,1)}, bf16[1024,1,256]{2,0,1:T(8,128)(2,1)}, u32[]{:S(2)}, u32[]{:S(2)}) collective-permute-start(bf16[1024,1,256]{2,0,1:T(8,128)(2,1)} %dynamic-slice_convert_fusion.2), channel_id=1, source_target_pairs={{0,2},{1,3},{2,0},{3,1},{4,6},{5,7},{6,4},{7,5},{8,10},{9,11},{10,... | collective-permute-start | bytes 1572872 | tf_op jit(solution)/shard_map/ppermute | solution.py:154
  523.2 8.4 %collective-permute-start.34 = (bf16[128,1024]{0,1:T(8,128)(2,1)}, bf16[128,1024]{0,1:T(8,128)(2,1)}, u32[]{:S(2)}, u32[]{:S(2)}) collective-permute-start(bf16[128,1024]{0,1:T(8,128)(2,1)} %get-tuple-element.89), channel_id=1, source_target_pairs={{0,8},{8,16},{16,24},{24,28},{28,20},{20,12},{12,4},{4,0},{1,9},{9... | collective-permute-start | bytes 786440 | tf_op jit(solution)/shard_map/ppermute | solution.py:145
  525.6 72.8 %collective-permute-start.38 = (bf16[128,1024]{0,1:T(8,128)(2,1)}, bf16[128,1024]{0,1:T(8,128)(2,1)S(1)}, u32[]{:S(2)}, u32[]{:S(2)}) collective-permute-start(bf16[128,1024]{0,1:T(8,128)(2,1)} %get-tuple-element.90), channel_id=1, source_target_pairs={{8,0},{16,8},{24,16},{28,24},{20,28},{12,20},{4,12},{0,4},{9,1},{1... | collective-permute-start | bytes 786440 | tf_op jit(solution)/shard_map/ppermute | solution.py:145
  533.3 56.4 %copy-start.81 = (f32[16,128]{1,0:T(8,128)S(1)}, f32[16,128]{1,0:T(8,128)}, u32[]{:S(2)}) copy-start(f32[16,128]{1,0:T(8,128)} %copy-done.80) | copy-start | bytes 24580
  533.3 56.4 %copy-start.83 = (f32[16,128]{1,0:T(8,128)S(1)}, f32[16,128]{1,0:T(8,128)}, u32[]{:S(2)}) copy-start(f32[16,128]{1,0:T(8,128)} %copy-done.82) | copy-start | bytes 24580
  533.3 58.3 %collective-permute-start.35 = (bf16[128,1024]{0,1:T(8,128)(2,1)}, bf16[128,1024]{0,1:T(8,128)(2,1)}, u32[]{:S(2)}, u32[]{:S(2)}) collective-permute-start(bf16[128,1024]{0,1:T(8,128)(2,1)} %add_convert_fusion.12), channel_id=1, source_target_pairs={{0,8},{8,16},{16,24},{24,28},{28,20},{20,12},{12,4},{4,0},{1,9},{9... | collective-permute-start | bytes 786440 | tf_op jit(solution)/shard_map/ppermute | solution.py:145
  538.4 81.8 %collective-permute-start.32 = (bf16[1024,2,256]{2,0,1:T(8,128)(2,1)}, bf16[1024,2,256]{2,0,1:T(8,128)(2,1)S(1)}, u32[]{:S(2)}, u32[]{:S(2)}) collective-permute-start(bf16[1024,2,256]{2,0,1:T(8,128)(2,1)} %dynamic-slice_bitcast_fusion), channel_id=1, source_target_pairs={{0,1},{1,0},{2,3},{3,2},{4,5},{5,4},{6,7},{7,6},{8,9},{9,8},{10,11... | collective-permute-start | bytes 3145736 | tf_op jit(solution)/shard_map/ppermute | solution.py:154
  592.6 7.8 %collective-permute-start.36 = (bf16[128,1024]{0,1:T(8,128)(2,1)S(1)}, bf16[128,1024]{0,1:T(8,128)(2,1)S(1)}, u32[]{:S(2)}, u32[]{:S(2)}) collective-permute-start(bf16[128,1024]{0,1:T(8,128)(2,1)S(1)} %add_convert_fusion.11), channel_id=1, source_target_pairs={{0,8},{8,16},{16,24},{24,28},{28,20},{20,12},{12,4},{4,0},{1,9},{9... | collective-permute-start | bytes 786440 | tf_op jit(solution)/shard_map/ppermute | solution.py:145
  600.6 19.4 %collective-permute-start.39 = (bf16[128,1024]{0,1:T(8,128)(2,1)S(1)}, bf16[128,1024]{0,1:T(8,128)(2,1)S(1)}, u32[]{:S(2)}, u32[]{:S(2)}) collective-permute-start(bf16[128,1024]{0,1:T(8,128)(2,1)S(1)} %get-tuple-element.88), channel_id=1, source_target_pairs={{8,0},{16,8},{24,16},{28,24},{20,28},{12,20},{4,12},{0,4},{9,1},{1... | collective-permute-start | bytes 786440 | tf_op jit(solution)/shard_map/ppermute | solution.py:145
  604.8 19.2 %collective-permute-start.37 = (bf16[128,1024]{0,1:T(8,128)(2,1)S(1)}, bf16[128,1024]{0,1:T(8,128)(2,1)S(1)}, u32[]{:S(2)}, u32[]{:S(2)}) collective-permute-start(bf16[128,1024]{0,1:T(8,128)(2,1)S(1)} %get-tuple-element.87), channel_id=1, source_target_pairs={{0,8},{8,16},{16,24},{24,28},{28,20},{20,12},{12,4},{4,0},{1,9},{9... | collective-permute-start | bytes 786440 | tf_op jit(solution)/shard_map/ppermute | solution.py:145
  620.1 20.3 %collective-permute-start.40 = (bf16[128,1024]{0,1:T(8,128)(2,1)S(1)}, bf16[128,1024]{0,1:T(8,128)(2,1)S(1)}, u32[]{:S(2)}, u32[]{:S(2)}) collective-permute-start(bf16[128,1024]{0,1:T(8,128)(2,1)S(1)} %add_convert_fusion.8), channel_id=1, source_target_pairs={{8,0},{16,8},{24,16},{28,24},{20,28},{12,20},{4,12},{0,4},{9,1},{1... | collective-permute-start | bytes 786440 | tf_op jit(solution)/shard_map/ppermute | solution.py:145
  621.9 18.5 %copy-start.24 = (f32[1024,2,256]{2,0,1:T(8,128)}, f32[1024,2,256]{2,0,1:T(8,128)S(1)}, u32[]{:S(2)}) copy-start(f32[1024,2,256]{2,0,1:T(8,128)S(1)} %maximum_add_fusion.5) | copy-start | bytes 6291460
  622.0 20.1 %collective-permute-start.33 = (bf16[1024,1,256]{2,0,1:T(8,128)(2,1)S(1)}, bf16[1024,1,256]{2,0,1:T(8,128)(2,1)S(1)}, u32[]{:S(2)}, u32[]{:S(2)}) collective-permute-start(bf16[1024,1,256]{2,0,1:T(8,128)(2,1)S(1)} %dynamic-slice_convert_fusion), channel_id=1, source_target_pairs={{0,2},{1,3},{2,0},{3,1},{4,6},{5,7},{6,4},{7,5},{8,10},{9,11},{10,... | collective-permute-start | bytes 1572872 | tf_op jit(solution)/shard_map/ppermute | solution.py:154
  (90 other events, 374.1 us)
Sparse Core Ops, SparseCore 0:
  35.8 79.3 all-gather.1
  466.3 123.3 all-reduce.2
  593.3 100.0 reduce-scatter.3
